TPU v7x, 512 devices: a whole 4x4x16 slice. The times are simulated.
512 devices in a mesh: sess: 16 (over z), tile: 32 (over y, x, core).
Axes of the slice: x: 4, y: 4, z: 16, core: 2. Of those that a mesh axis runs over, the one named last changes fastest.
Arguments:
- features: bfloat16 [96, 64, 320, 128], P('sess', 'tile'), parts along dimension 0, may hold values from -6 to 6
- dec_weight: bfloat16 [9, 128, 128], replicated, may hold values from -0.1875 to 0.1875
- dec_bias: float32 [128], replicated, may hold values from -3 to 3
- first_weight: bfloat16 [9, 128, 128], replicated, may hold values from -0.1875 to 0.1875
- first_bias: float32 [128], replicated, may hold values from -3 to 3
- second_weight: bfloat16 [9, 128, 128], replicated, may hold values from -0.1875 to 0.1875
- second_bias: float32 [128], replicated, may hold values from -3 to 3
- boxes: int32 [3, 512], P(None, 'sess'), parts along dimension 1, may hold values from 0 to 336, as said below
- slots: int32 [1024], P('sess'), parts along dimension 0, may hold values from -1 to 31, as said below
Outputs:
- finished: bfloat16 [96, 64, 320, 128], P('sess', 'tile'), parts along dimension 0
- restorations: bfloat16 [1024, 64, 64, 128], P(('sess', 'tile')), parts along dimension 0
There are 16 independent parts, one for each index of `sess`. A program takes and returns all parts, laid end to end along the dimension named above; an argument that names none is the same for every part. Nothing has to cross between parts.
Inputs may be any that keep to these rules, and one draw needn't show every extreme that they name: Column k of boxes is crop k: its first row r, its first column w and its size class c; the box has side 12 * (c + 2), and the square of side 48 at rows r, columns w lies inside the frame; some crop has class 3 - 1. `slots`: entries w * 2 to w * 2 + 1 are the crops that worker w restores, -1 marking an empty entry; each crop appears exactly once; some worker has 2 crops.
All inputs are finite; a program needn't handle non-finite values.
Results may differ from a plain program's by a relative error of at most 0.0057.
Values may be sent and summed in bfloat16 or wider, within the bound.
A program may use at most 64 MiB of HBM per device.

v0:
```python
import jax
import jax.numpy as jnp
from jax import lax
from jax.sharding import PartitionSpec as P

S = 64
UNIT = 12
NCLS = 3
CAP = 2


def extended_2(x, sides, width):
    for axis, dim in sides:
        peers, length = (lax.axis_size(axis), x.shape[dim])
        up = [(i, (i + 1) % peers) for i in range(peers)]
        down = [(j, i) for i, j in up]
        last = lax.slice_in_dim(x, length - width, length, axis=dim)
        leading = lax.slice_in_dim(x, 0, width, axis=dim)
        before = lax.ppermute(last, axis, up)
        after = lax.ppermute(leading, axis, down)
        x = jnp.concatenate([before, x, after], axis=dim)
    return x


def hat_down(length, cells, size_out):
    lenf = length.astype(jnp.float32)
    spots = (jnp.arange(size_out, dtype=jnp.float32) + 0.5) * lenf / size_out - 0.5
    spots = jnp.clip(spots, 0.0, lenf - 1.0)
    return jnp.maximum(0.0, 1.0 - jnp.abs(spots[:, None] - cells[None, :]))


def hat_up(length, cells, size_in):
    lenf = length.astype(jnp.float32)
    spots = (cells + 0.5) * size_in / lenf - 0.5
    spots = jnp.clip(spots, 0.0, size_in - 1.0)
    inside = ((cells >= 0.0) & (cells < lenf)).astype(jnp.float32)
    grid = jnp.arange(size_in, dtype=jnp.float32)
    return jnp.maximum(0.0, 1.0 - jnp.abs(spots[:, None] - grid[None, :])) * inside[:, None]


def conv_taps(padded, weight):
    height = padded.shape[-3] - 2
    width = padded.shape[-2] - 2
    chans = padded.shape[-1]
    wide = jnp.concatenate(
        [padded[..., 0:width, :], padded[..., 1 : width + 1, :], padded[..., 2 : width + 2, :]],
        axis=-1,
    )
    stacked = weight.reshape(3, 3 * chans, weight.shape[-1])
    total = None
    for offset in range(3):
        term = jnp.einsum(
            "...hwk,kd->...hwd",
            wide[..., offset : offset + height, :, :],
            stacked[offset],
            preferred_element_type=jnp.float32,
        )
        total = term if total is None else total + term
    return total


def shards(
    features,
    dec_weight,
    dec_bias,
    first_weight,
    first_bias,
    second_weight,
    second_bias,
    boxes,
    slots,
):
    bands, band_rows, cols, chans = features.shape
    tile_count = lax.axis_size("tile")
    position = lax.axis_index("tile")
    span = UNIT * (NCLS + 1)
    stride = tile_count * band_rows
    piece = band_rows * (span // stride + 1)
    local_rows = bands * band_rows
    highest = lax.Precision.HIGHEST
    anchor = jnp.zeros((), jnp.int32)
    grown = extended_2(features, (("tile", 1),), 1)
    upper_rim = grown[:, 0]
    lower_rim = grown[:, band_rows + 1]
    blank_rim = jnp.zeros_like(upper_rim[:1])
    upper_rim = jnp.where(position == 0, jnp.concatenate([blank_rim, upper_rim[:-1]], 0), upper_rim)
    lower_rim = jnp.where(
        position == tile_count - 1, jnp.concatenate([lower_rim[1:], blank_rim], 0), lower_rim
    )
    extended = jnp.concatenate([upper_rim[:, None], features, lower_rim[:, None]], axis=1)
    extended = jnp.pad(extended, ((0, 0), (0, 0), (1, 1), (0, 0)))
    decoded = (
        features.astype(jnp.float32) + jax.nn.silu(conv_taps(extended, dec_weight) + dec_bias)
    ).astype(jnp.bfloat16)
    decoded = decoded.reshape(local_rows, cols, chans)
    widened = jnp.pad(decoded, ((0, piece), (0, span), (0, 0)))
    band_index = jnp.arange(bands, dtype=jnp.int32)[:, None] * stride
    within = position * band_rows + jnp.arange(band_rows, dtype=jnp.int32)[None, :]
    global_rows = (band_index + within).reshape(local_rows)
    padded_rows = jnp.concatenate(
        [global_rows, jnp.full((piece,), stride * bands + span, jnp.int32)]
    )
    box_cells = jnp.arange(span, dtype=jnp.float32)

    def locate(slot):
        crop = jnp.maximum(slot, 0)
        row0 = boxes[0, crop]
        col0 = boxes[1, crop]
        length = UNIT * (boxes[2, crop] + 2)
        start = jnp.sum((global_rows < row0).astype(jnp.int32))
        offsets = lax.dynamic_slice_in_dim(padded_rows, start, piece) - row0
        valid = (offsets < span) & (slot >= 0)
        return (start, col0, length, offsets, valid)

    def outgoing(slot):
        start, col0, length, offsets, valid = locate(slot)
        block = lax.dynamic_slice(widened, (start, col0, anchor), (piece, span, chans))
        block = jnp.where(valid[:, None, None], block, jnp.zeros_like(block))
        across = hat_down(length, box_cells, S)
        payload = jnp.einsum(
            "tw,rwc->rtc", across, block.astype(jnp.float32), precision=highest
        ).astype(jnp.bfloat16)
        places = jnp.where(valid, offsets, -1).astype(jnp.float32)
        size_entry = jnp.where(slot >= 0, length, span).astype(jnp.float32)
        meta = jnp.concatenate([places, size_entry[None]]).astype(jnp.bfloat16)
        return (payload, meta)

    sent, meta = lax.map(outgoing, slots)
    sent = sent.reshape((tile_count, CAP) + sent.shape[1:])
    meta = meta.reshape(tile_count, CAP, piece + 1)

    def restore_one(crop):
        padded = jnp.pad(crop, ((1, 1), (1, 1), (0, 0)))
        inner = jax.nn.silu(conv_taps(padded, first_weight) + first_bias).astype(jnp.bfloat16)
        padded = jnp.pad(inner, ((1, 1), (1, 1), (0, 0)))
        return (conv_taps(padded, second_weight) + second_bias).astype(jnp.bfloat16)

    got_rows = lax.all_to_all(sent, "tile", split_axis=0, concat_axis=0, tiled=True)
    got_meta = lax.all_to_all(meta, "tile", split_axis=0, concat_axis=0, tiled=True)
    sources = got_rows.shape[0]
    count = got_rows.shape[1]
    places = jnp.transpose(got_meta[:, :, :piece].astype(jnp.float32), (1, 0, 2)).reshape(
        count, sources * piece
    )
    lengths = got_meta[0, :, piece].astype(jnp.float32)
    down_rows = jax.vmap(lambda size_one, cell_one: hat_down(size_one, cell_one, S))(
        lengths, places
    )
    down_rows = down_rows.reshape(count, S, sources, piece)
    crops = jnp.einsum(
        "mser,emrtc->mstc", down_rows, got_rows.astype(jnp.float32), precision=highest
    ).astype(jnp.bfloat16)
    delta = lax.map(restore_one, crops)
    lifts = jax.vmap(lambda size_one, cell_one: hat_up(size_one, cell_one, S))(lengths, places)
    lifts = lifts.reshape(count, sources, piece, S)
    upper = jnp.einsum(
        "mers,mstc->emrtc", lifts, delta.astype(jnp.float32), precision=highest
    ).astype(jnp.bfloat16)
    finish_returned = lax.all_to_all(upper, "tile", split_axis=0, concat_axis=0, tiled=True)
    returned = finish_returned
    deltas = delta[None]
    returned = returned.reshape((tile_count * CAP,) + returned.shape[2:])
    owned = lax.dynamic_slice_in_dim(slots, position * CAP, CAP)
    keep = (owned >= 0)[:, None, None, None]
    restorations = jnp.where(keep, deltas[0], jnp.zeros_like(deltas[0]))

    def paste_slot(index, canvas):
        start, col0, length, offsets, valid = locate(slots[index])
        incoming = returned[index]
        lift = hat_up(length, box_cells, S)
        patch = jnp.einsum(
            "wt,rtc->rwc", lift, incoming.astype(jnp.float32), precision=highest
        ).astype(jnp.bfloat16)
        old = lax.dynamic_slice(canvas, (start, col0, anchor), (piece, span, chans))
        return lax.dynamic_update_slice(
            canvas, old + patch.astype(jnp.float32), (start, col0, anchor)
        )

    canvas = lax.fori_loop(
        0,
        tile_count * CAP,
        paste_slot,
        jnp.zeros((local_rows + piece, cols + span, chans), jnp.float32),
    )
    finished = (decoded.astype(jnp.float32) + canvas[:local_rows, :cols]).astype(jnp.bfloat16)
    return (finished.reshape(bands, band_rows, cols, chans), restorations)


def solution(mesh):
    return jax.shard_map(
        shards,
        mesh=mesh,
        in_specs=(
            P("sess", "tile", None, None),
            P(),
            P(),
            P(),
            P(),
            P(),
            P(),
            P(None, "sess"),
            P("sess"),
        ),
        out_specs=(P("sess", "tile", None, None), P(("sess", "tile"), None, None, None)),
        check_vma=False,
    )
```

profile of v0, /device:TPU:1, one launch (start us, length us, event | category | flops | bytes accessed | tf_op | source)
XLA Modules:
  0.0 1434.2 jit_solution(6135934885011263462)
XLA Ops:
  0.6 2.2 slice_bitcast_fusion.1
  2.9 8.7 collective-permute-start.1
  11.6 1.9 collective-permute-start
  14.1 5.5 collective-permute-done
  24.3 1.3 add_convert_fusion.2
  26.7 701.4 %while.48 = (s32[]{:T(128)}, bf16[64,2,64,128]{3,2,1,0:T(8,128)(2,1)S(1)}, bf16[64,3]{1,0:T(8,128)(2,1)}, s32[64]{0:T(128)S(1)}, s32[3,32]{1,0:T(4,128)S(1)}, /*...) while((s32[]{:T(128)}, ...), condition=%wide.region_2.3_spmd.clone.clone, body=%wide.region_0.2_spmd.clone.sunk.clone | while | flops 9478615 | bytes 59236 | solution.py:128
  299.5 1.3 dynamic_update_slice.47
  310.4 1.3 dynamic_update_slice.47
  321.4 1.3 dynamic_update_slice.47
  728.2 9.2 all-to-all-start
  737.4 3.5 copy.54
  740.9 3.6 all-to-all-done
  744.4 5.0 all-to-all-start.1
  750.0 27.7 %all-to-all-done.1 = bf16[32,2,2,64,128]{4,2,3,1,0:T(2,128)(2,1)} async-done(((bf16[32,2,2,64,128]{4,2,3,1,0:T(2,128)(2,1)}), bf16[32,2,2,64,128]{4,2,3,1,0:T(2,128)(2,1)}, u32[]{:S(2)}, u32[]{:S(2)}) %all-to-all-start.1) | async-done | bytes 2097184 | tf_op jit(solution)/shard_map/all_to_all | solution.py:138
  777.7 4.3 bitcast_convert_fusion
  782.1 22.4 %while.47 = (s32[]{:T(128)}, bf16[2,64,64,128]{3,2,1,0:T(8,128)(2,1)}, bf16[2,64,64,128]{3,1,2,0:T(8,128)(2,1)S(1)}, bf16[9,128,128]{2,1,0:T(8,128)(2,1)S(1)}, f...) while((s32[]{:T(128)}, bf16[2,64,64,128]{3,2,1,0:T(8,128)(2,1)}, ...), condition=%wide.region_4.5_spmd.clone, body=%wide.region_3.4_spmd.sunk.clone | while | flops 2480603136 | bytes 52889168 | solution.py:153
  782.9 1.5 pad_slice_fusion.10
  786.4 1.5 multiply_convert_fusion.3
  787.8 1.5 pad_slice_fusion.11
  791.3 2.0 fusion.165
  794.1 1.5 pad_slice_fusion.10
  797.5 1.5 multiply_convert_fusion.3
  799.0 1.5 pad_slice_fusion.11
  802.4 2.0 fusion.165
  804.5 4.2 convert_bitcast_fusion.1
  808.7 3.6 copy.58
  812.4 5.9 all-to-all-start.2
  818.3 3.1 broadcast_select_fusion
  821.4 25.1 %all-to-all-done.2 = bf16[32,2,2,64,128]{4,2,3,1,0:T(2,128)(2,1)S(1)} async-done(((bf16[32,2,2,64,128]{4,2,3,1,0:T(2,128)(2,1)}), bf16[32,2,2,64,128]{4,2,3,1,0:T(2,128)(2,1)S(1)}, u32[]{:S(2)}, u32[]{:S(2)}) %all-to-all-start.2) | async-done | bytes 2097184 | tf_op jit(solution)/shard_map/all_to_all | solution.py:159
  846.5 1.9 copy.59
  848.6 583.1 %while.49 = (s32[]{:T(128)}, f32[14,368,128]{2,1,0:T(8,128)S(1)}, s32[64]{0:T(128)S(1)}, s32[3,32]{1,0:T(4,128)S(1)}, bf16[64,2,64,128]{3,2,1,0:T(8,128)(2,1)}, ...) while((s32[]{:T(128)}, f32[14,368,128]{2,1,0:T(8,128)S(1)}, ...), condition=%wide.region_7.8_spmd.clone.clone.clone, body=%wide.region_5.7_spmd.clone.clone.sunk.clone | while | flops 9489803 | bytes 231161 | solution.py:179
  1431.8 2.4 add_convert_fusion.1
  (1277 shorter events, 586.9 us)
Async XLA Ops:
  0.6 13.1 copy-start.4
  2.9 11.2 collective-permute-start.1
  11.6 8.0 collective-permute-start
  13.8 6.0 copy-start
  23.3 1.0 copy-start.6
  25.6 1.0 copy-start.3
  25.7 1.1 copy-start.5
  25.7 1.1 copy-start.9
  728.2 16.3 %all-to-all-start = ((bf16[32,2,3]{2,1,0:T(2,128)(2,1)}), bf16[32,2,3]{2,1,0:T(2,128)(2,1)S(1)}, u32[]{:S(2)}, u32[]{:S(2)}) async-start(bf16[32,2,3]{2,1,0:T(2,128)(2,1)} %bitcast.30), calls=%async_computation | async-start | bytes 32768 | tf_op jit(solution)/shard_map/all_to_all | solution.py:139
  744.4 33.3 %all-to-all-start.1 = ((bf16[32,2,2,64,128]{4,2,3,1,0:T(2,128)(2,1)}), bf16[32,2,2,64,128]{4,2,3,1,0:T(2,128)(2,1)}, u32[]{:S(2)}, u32[]{:S(2)}) async-start(bf16[32,2,2,64,128]{4,2,3,1,0:T(2,128)(2,1)} %copy.54), calls=%async_computation.1 | async-start | bytes 4194304 | tf_op jit(solution)/shard_map/all_to_all | solution.py:138
  750.0 32.1 %copy-start.1 = (bf16[9,128,128]{2,1,0:T(8,128)(2,1)S(1)}, bf16[9,128,128]{2,1,0:T(8,128)(2,1)}, u32[]{:S(2)}) copy-start(bf16[9,128,128]{2,1,0:T(8,128)(2,1)} %param.18) | copy-start | bytes 884740
  750.0 32.1 %copy-start.2 = (bf16[9,128,128]{2,1,0:T(8,128)(2,1)S(1)}, bf16[9,128,128]{2,1,0:T(8,128)(2,1)}, u32[]{:S(2)}) copy-start(bf16[9,128,128]{2,1,0:T(8,128)(2,1)} %param.20) | copy-start | bytes 884740
  750.0 32.1 %copy-start.7 = (f32[128]{0:T(128)S(1)}, f32[128]{0:T(128)}, u32[]{:S(2)}) copy-start(f32[128]{0:T(128)} %param.19) | copy-start | bytes 1540
  750.0 32.1 %copy-start.8 = (f32[128]{0:T(128)S(1)}, f32[128]{0:T(128)}, u32[]{:S(2)}) copy-start(f32[128]{0:T(128)} %param.21) | copy-start | bytes 1540
  812.4 34.2 %all-to-all-start.2 = ((bf16[32,2,2,64,128]{4,2,3,1,0:T(2,128)(2,1)}), bf16[32,2,2,64,128]{4,2,3,1,0:T(2,128)(2,1)S(1)}, u32[]{:S(2)}, u32[]{:S(2)}) async-start(bf16[32,2,2,64,128]{4,2,3,1,0:T(2,128)(2,1)} %copy.58), calls=%async_computation.2 | async-start | bytes 4194304 | tf_op jit(solution)/shard_map/all_to_all | solution.py:159
where the time goes:
time: 1450 us; the launch traced here: 1430 us
  loops' own time  710 us (49%)
  local copies, waits for them, and re-layouts  293 us (20%)
  other arithmetic  231 us (16%)
  matrix products  107 us (7%)
  waiting for transfers between devices  62.2 us (4%)
  starting transfers between devices  30.7 us (2%)
    another operation x1, loops' own time, shards(): sent, meta = lax.map(outgoing, slots)  382 us
    another operation x1, loops' own time, shards(): lax.fori_loop(0, tile_count * CAP, paste_slot, jnp.zeros((local_rows + pi...  328 us
    reduce_sum x128, other arithmetic, locate(): start = jnp.sum((global_rows < row0).astype(jnp.int32))  161 us
    dynamic_slice x128, local copies, waits for them, and re-layouts, locate(): length = UNIT * (boxes[2, crop] + 2)  84.9 us
    dynamic_update_slice x64, local copies, waits for them, and re-layouts, shards(): sent, meta = lax.map(outgoing, slots)  81 us
    dot_general x64, matrix products, paste_slot(): jnp.einsum('wt,rtc->rwc', lift, incoming.astype(jnp.float32), precision=h...  63.5 us
    concatenate x128, other arithmetic, outgoing(): meta = jnp.concatenate([places, size_entry[None]]).astype(jnp.bfloat16)  50.6 us
    dynamic_slice x64, local copies, waits for them, and re-layouts, paste_slot(): start, col0, length, offsets, valid = locate(slots[index])  37.7 us
  transfers between devices with their start and end apart: 5, of which 5 were waited for; matrix products, arithmetic and copies ran while one was open for 1% of the time, Pallas kernels for 0%

commit v1 on v0

v1 whole, which is shorter than its diff:
```python
import functools

import jax
import jax.numpy as jnp
from jax import lax
from jax.experimental import pallas as pl
from jax.experimental.pallas import tpu as pltpu
from jax.sharding import PartitionSpec as P

S = 64
UNIT = 12
SPAN = 48
C = 128
BANDS = 6
COLS = 320
STRIDE = 64
TILES = 32
CAP = 2
MESH = pl.DeviceIdType.MESH
BF = jnp.bfloat16
F32 = jnp.float32

OFFSETS = sorted(
    [(dy, dx, dc) for dy in range(4) for dx in range(4) for dc in range(2) if dy + dx + dc],
    key=lambda d: -(min(d[0], 4 - d[0]) + min(d[1], 4 - d[1])),
)


def silu(v):
    return v * (1.0 / (1.0 + jnp.exp(-v)))


def rounded(v):
    return v.astype(BF).astype(F32)


def pair_weight(w_ref, out_ref):
    zero = jnp.zeros((C, C), BF)
    for a in range(4):
        for dx in range(3):
            rows = pl.ds((a * 3 + dx) * C, C)
            out_ref[rows, 0:C] = w_ref[3 * a + dx] if a < 3 else zero
            out_ref[rows, C : 2 * C] = w_ref[3 * (a - 1) + dx] if a > 0 else zero


def widen(pad_ref, index, cols):
    return jnp.concatenate(
        [pad_ref[index, pl.ds(7 + dx, cols), :].astype(BF) for dx in range(3)], axis=-1
    )


def side_of(boxes, crop):
    return UNIT * (boxes[2, crop] + 2)


def decode_kernel(
    boxes, slots, feat, above, below, w_ref, b_ref, dec, payload, w_pair, pad, wide, held
):
    position = lax.axis_index("tile")
    pair_weight(w_ref, w_pair)
    pad[:, 0:8, :] = jnp.zeros((4, 8, C), F32)
    pad[:, COLS + 8 : COLS + 16, :] = jnp.zeros((4, 8, C), F32)
    bias = jnp.concatenate([b_ref[...], b_ref[...]], axis=-1)

    def band(b, _):
        up = jnp.where(position == 0, b - 1, b)
        down = jnp.where(position == TILES - 1, b + 1, b)
        up_ok = (up >= 0).astype(F32)
        down_ok = (down < BANDS).astype(F32)
        pad[0, 8 : COLS + 8, :] = above[jnp.maximum(up, 0)].astype(F32) * up_ok
        pad[1, 8 : COLS + 8, :] = feat[b, 0].astype(F32)
        pad[2, 8 : COLS + 8, :] = feat[b, 1].astype(F32)
        pad[3, 8 : COLS + 8, :] = below[jnp.minimum(down, BANDS - 1)].astype(F32) * down_ok
        for a in range(4):
            wide[a] = widen(pad, a, COLS)
        for part in range(2):
            rows = pl.ds(part * (COLS // 2), COLS // 2)
            lhs = jnp.concatenate([wide[a, rows, :] for a in range(4)], axis=-1)
            acc = jnp.dot(lhs, w_pair[...], preferred_element_type=F32) + bias
            act = silu(acc)
            for o in range(2):
                v = (feat[b, o, rows, :].astype(F32) + act[:, o * C : (o + 1) * C]).astype(BF)
                dec[b, o, rows, :] = v
                held[2 * b + o, rows, :] = v.astype(F32)
        return 0

    lax.fori_loop(0, BANDS, band, 0)

    def fill(q, _):
        crop = jnp.maximum(slots[q], 0)
        row0 = boxes[0, crop]
        col0 = boxes[1, crop]
        for i in range(2):
            h = (2 * position + i - row0) & (STRIDE - 1)
            row = 2 * jnp.minimum((row0 + h) >> 6, BANDS - 1) + i
            payload[q, i] = held[row, pl.ds(col0, SPAN), :].astype(BF)
        return 0

    lax.fori_loop(0, TILES * CAP, fill, 0, unroll=2)


def exchange_kernel(src, dst, send_sem, recv_sem, own_sem):
    me = lax.axis_index("tile")
    y, x, core = me // 8, (me // 2) % 4, me % 2
    targets = [
        ((y + dy) % 4) * 8 + ((x + dx) % 4) * 2 + (core + dc) % 2 for dy, dx, dc in OFFSETS
    ]
    barrier = pltpu.get_barrier_semaphore()
    for t in targets:
        pl.semaphore_signal(barrier, inc=1, device_id={"tile": t}, device_id_type=MESH)
    own = pltpu.make_async_copy(src.at[me], dst.at[me], own_sem)
    own.start()
    pl.semaphore_wait(barrier, TILES - 1)
    copies = [
        pltpu.make_async_remote_copy(
            src_ref=src.at[t],
            dst_ref=dst.at[me],
            send_sem=send_sem.at[k],
            recv_sem=recv_sem.at[k],
            device_id={"tile": t},
            device_id_type=MESH,
        )
        for k, t in enumerate(targets)
    ]
    for copy in copies:
        copy.start()
    own.wait()
    for copy in copies:
        copy.wait()


def exchange(x, collective_id):
    n = len(OFFSETS)
    return pl.pallas_call(
        exchange_kernel,
        out_shape=jax.ShapeDtypeStruct(x.shape, x.dtype),
        in_specs=[pl.BlockSpec(memory_space=pl.ANY)],
        out_specs=pl.BlockSpec(memory_space=pl.ANY),
        scratch_shapes=[
            pltpu.SemaphoreType.DMA((n,)),
            pltpu.SemaphoreType.DMA((n,)),
            pltpu.SemaphoreType.DMA,
        ],
        compiler_params=pltpu.CompilerParams(collective_id=collective_id, has_side_effects=True),
        name=f"exchange_{collective_id}",
    )(x)


CHUNK = 4


def conv_pairs(wide, w_pair, bias, m0):
    lhs = jnp.concatenate(
        [
            wide[pl.ds(m0 + a // 2, CHUNK), a % 2].reshape(CHUNK * S, 3 * C)
            for a in range(4)
        ],
        axis=-1,
    )
    return jnp.dot(lhs, w_pair[...], preferred_element_type=F32) + bias


def restore_kernel(
    boxes, slots, got, w1, b1, w2, b2, rest, back, w1_pair, w2_pair, cut, pad, wide, wide2, delta
):
    step = pl.program_id(0)
    position = lax.axis_index("tile")

    @pl.when(step == 0)
    def _():
        pair_weight(w1, w1_pair)
        pair_weight(w2, w2_pair)
        pad[:, 0:8, :] = jnp.zeros((S, 8, C), F32)
        pad[:, S + 8 : S + 16, :] = jnp.zeros((S, 8, C), F32)
        for ref in (wide, wide2):
            ref[0, 0] = jnp.zeros((S, 3 * C), BF)
            ref[S // 2, 1] = jnp.zeros((S, 3 * C), BF)

    slot = slots[CAP * position + step]
    crop = jnp.maximum(slot, 0)
    row0 = boxes[0, crop]
    side = side_of(boxes, crop)
    sidef = side.astype(F32)

    spot = (lax.broadcasted_iota(jnp.int32, (S, SPAN), 0).astype(F32) + 0.5) * sidef / S - 0.5
    spot = jnp.clip(spot, 0.0, sidef - 1.0)
    cell = lax.broadcasted_iota(jnp.int32, (S, SPAN), 1).astype(F32)
    down = jnp.maximum(0.0, 1.0 - jnp.abs(spot - cell)).astype(BF)

    def colcut(p, _):
        rhs = jnp.concatenate([got[p, 0, 0], got[p, 0, 1]], axis=-1)
        y = rounded(jnp.dot(down, rhs, preferred_element_type=F32))
        cut[2 * p] = y[:, 0:C]
        cut[2 * p + 1] = y[:, C : 2 * C]
        return 0

    lax.fori_loop(0, TILES, colcut, 0, unroll=4)

    def crop_row(s, _):
        num = jnp.clip((2 * s + 1) * side - S, 0, (side - 1) * 128)
        first = num >> 7
        second = jnp.minimum(first + 1, SPAN - 1)
        frac = (num & 127).astype(F32) * (1.0 / 128.0)
        a = cut[(row0 + first) & (STRIDE - 1)]
        b = cut[(row0 + second) & (STRIDE - 1)]
        pad[s, 8 : S + 8, :] = rounded((1.0 - frac) * a + frac * b)
        return 0

    lax.fori_loop(0, S, crop_row, 0, unroll=4)

    def spread(target):
        def body(s, _):
            target[(s + 1) >> 1, (s + 1) & 1] = widen(pad, s, S)
            return 0

        lax.fori_loop(0, S, body, 0, unroll=4)

    spread(wide)
    bias1 = jnp.concatenate([b1[...], b1[...]], axis=-1)
    bias2 = jnp.concatenate([b2[...], b2[...]], axis=-1)

    def first(j, _):
        v = rounded(silu(conv_pairs(wide, w1_pair, bias1, j * CHUNK)))
        v = v.reshape(CHUNK, S, 2 * C)
        for i in range(CHUNK):
            for o in range(2):
                pad[2 * (j * CHUNK + i) + o, 8 : S + 8, :] = v[i, :, o * C : (o + 1) * C]
        return 0

    lax.fori_loop(0, S // 2 // CHUNK, first, 0)
    spread(wide2)
    keep = slot >= 0

    def second(j, _):
        v = rounded(conv_pairs(wide2, w2_pair, bias2, j * CHUNK))
        v = v.reshape(CHUNK, S, 2 * C)
        for i in range(CHUNK):
            for o in range(2):
                row = 2 * (j * CHUNK + i) + o
                part = v[i, :, o * C : (o + 1) * C]
                delta[row] = part
                rest[0, row] = jnp.where(keep, part, 0.0).astype(BF)
        return 0

    lax.fori_loop(0, S // 2 // CHUNK, second, 0)

    where = (lax.broadcasted_iota(jnp.int32, (SPAN, S), 0).astype(F32) + 0.5) * S / sidef - 0.5
    where = jnp.clip(where, 0.0, S - 1.0)
    inside = lax.broadcasted_iota(jnp.int32, (SPAN, S), 0) < side
    grid = lax.broadcasted_iota(jnp.int32, (SPAN, S), 1).astype(F32)
    lift = jnp.where(inside, jnp.maximum(0.0, 1.0 - jnp.abs(where - grid)), 0.0)
    lift_high = lift.astype(BF)
    lift_low = (lift - lift_high.astype(F32)).astype(BF)
    lifts = jnp.concatenate([lift_high, lift_low], axis=-1)
    magic = jnp.where(side == 24, 10923, jnp.where(side == 36, 7282, 5462))

    def patch(p, _):
        halves = []
        for i in range(2):
            h = (2 * p + i - row0) & (STRIDE - 1)
            num = jnp.clip((2 * h + 1) * (S // 2) - (side >> 1), 0, (S - 1) * side)
            one = (num * magic) >> 18
            frac = (num - one * side).astype(F32) / sidef
            live = (h < side).astype(F32)
            two = jnp.minimum(one + 1, S - 1)
            halves.append(
                ((live * (1.0 - frac)) * delta[one] + (live * frac) * delta[two]).astype(BF)
            )
        rhs = jnp.concatenate(halves, axis=-1)
        rhs = jnp.concatenate([rhs, rhs], axis=0)
        y = jnp.dot(lifts, rhs, preferred_element_type=F32).astype(BF)
        back[p, 0, 0] = y[:, 0:C]
        back[p, 0, 1] = y[:, C : 2 * C]
        return 0

    lax.fori_loop(0, TILES, patch, 0, unroll=4)


def paste_kernel(boxes, slots, dec, back, out, acc):
    position = lax.axis_index("tile")
    for b in range(BANDS):
        for o in range(2):
            acc[2 * b + o] = dec[b, o].astype(F32)

    def body(q, _):
        slot = slots[q]
        crop = jnp.maximum(slot, 0)
        row0 = boxes[0, crop]
        cols = pl.ds(boxes[1, crop], SPAN)
        for i in range(2):
            h = (2 * position + i - row0) & (STRIDE - 1)
            live = (slot >= 0) & (h < SPAN)
            row = jnp.where(live, 2 * ((row0 + h) >> 6) + i, 2 * BANDS + i)
            acc[row, cols, :] = acc[row, cols, :] + back[q, i].astype(F32)
        return 0

    lax.fori_loop(0, TILES * CAP, body, 0, unroll=2)
    for b in range(BANDS):
        for o in range(2):
            out[b, o] = acc[2 * b + o].astype(BF)


def shards(
    features,
    dec_weight,
    dec_bias,
    first_weight,
    first_bias,
    second_weight,
    second_bias,
    boxes,
    slots,
):
    ring = [(i, (i + 1) % TILES) for i in range(TILES)]
    above = lax.ppermute(features[:, 1], "tile", ring)
    below = lax.ppermute(features[:, 0], "tile", [(j, i) for i, j in ring])
    smem = pl.BlockSpec(memory_space=pltpu.SMEM)
    vmem = pl.BlockSpec(memory_space=pltpu.VMEM)
    limit = 60 * 1024 * 1024
    rows = (TILES * CAP, 2, SPAN, C)

    decoded, payload = pl.pallas_call(
        decode_kernel,
        out_shape=(
            jax.ShapeDtypeStruct(features.shape, BF),
            jax.ShapeDtypeStruct(rows, BF),
        ),
        in_specs=[smem, smem] + [vmem] * 5,
        out_specs=(vmem, vmem),
        scratch_shapes=[
            pltpu.VMEM((12 * C, 2 * C), BF),
            pltpu.VMEM((4, COLS + 16, C), F32),
            pltpu.VMEM((4, COLS, 3 * C), BF),
            pltpu.VMEM((2 * BANDS, COLS, C), F32),
        ],
        compiler_params=pltpu.CompilerParams(vmem_limit_bytes=limit),
        name="decode",
    )(boxes, slots, features, above, below, dec_weight, dec_bias[None])

    blocks = (TILES, CAP, 2, SPAN, C)
    got = exchange(payload.reshape(blocks), 0)

    const = lambda shape: pl.BlockSpec(shape, lambda s: (0,) * len(shape))
    rest, back = pl.pallas_call(
        restore_kernel,
        grid=(CAP,),
        out_shape=(
            jax.ShapeDtypeStruct((CAP, S, S, C), BF),
            jax.ShapeDtypeStruct(blocks, BF),
        ),
        in_specs=[
            smem,
            smem,
            pl.BlockSpec((TILES, 1, 2, SPAN, C), lambda s: (0, s, 0, 0, 0)),
            const((9, C, C)),
            const((1, C)),
            const((9, C, C)),
            const((1, C)),
        ],
        out_specs=(
            pl.BlockSpec((1, S, S, C), lambda s: (s, 0, 0, 0)),
            pl.BlockSpec((TILES, 1, 2, SPAN, C), lambda s: (0, s, 0, 0, 0)),
        ),
        scratch_shapes=[
            pltpu.VMEM((12 * C, 2 * C), BF),
            pltpu.VMEM((12 * C, 2 * C), BF),
            pltpu.VMEM((S, S, C), F32),
            pltpu.VMEM((S, S + 16, C), F32),
            pltpu.VMEM((S // 2 + 1, 2, S, 3 * C), BF),
            pltpu.VMEM((S // 2 + 1, 2, S, 3 * C), BF),
            pltpu.VMEM((S, S, C), F32),
        ],
        compiler_params=pltpu.CompilerParams(vmem_limit_bytes=limit),
        name="restore",
    )(boxes, slots, got, first_weight, first_bias[None], second_weight, second_bias[None])

    returned = exchange(back, 1)
    finished = pl.pallas_call(
        paste_kernel,
        out_shape=jax.ShapeDtypeStruct(features.shape, BF),
        in_specs=[smem, smem, vmem, vmem],
        out_specs=vmem,
        scratch_shapes=[pltpu.VMEM((2 * BANDS + 2, COLS, C), F32)],
        compiler_params=pltpu.CompilerParams(vmem_limit_bytes=limit),
        name="paste",
    )(boxes, slots, decoded, returned.reshape(rows))
    return finished, rest


def solution(mesh):
    return jax.shard_map(
        shards,
        mesh=mesh,
        in_specs=(
            P("sess", "tile", None, None),
            P(),
            P(),
            P(),
            P(),
            P(),
            P(),
            P(None, "sess"),
            P("sess"),
        ),
        out_specs=(P("sess", "tile", None, None), P(("sess", "tile"), None, None, None)),
        check_vma=False,
    )
```

time: 1450 us -> 110 us (0.08); the launches traced: 1430 us -> 110 us
  loops' own time: 710 us -> 0 us
  local copies, waits for them, and re-layouts: 293 us -> 2.03 us
  other arithmetic: 231 us -> 0 us
  matrix products: 107 us -> 0 us
  Pallas kernels: 0 us -> 90.5 us
  waiting for transfers between devices: 62.2 us -> 5.75 us
  starting transfers between devices: 30.7 us -> 10.7 us
    another operation x3 -> x0, loops' own time: 710 us -> none  [the longest x1 382 us: shards(): sent, meta = lax.map(outgoing, slots)]
    reduce_sum x128 -> x0, other arithmetic: 161 us -> none  [locate(): start = jnp.sum((global_rows < row0).astype(jnp.int32))]
    dynamic_slice x260 -> x0, local copies, waits for them, and re-layouts: 161 us -> none  [the longest x128 84.9 us: locate(): length = UNIT * (boxes[2, crop] + 2)]
    dot_general x145 -> x0, matrix products: 107 us -> none  [the longest x64 63.5 us: paste_slot(): jnp.einsum('wt,rtc->rwc', lift, incoming.astype(jnp.float32), precision=h...]
    dynamic_update_slice x128 -> x0, local copies, waits for them, and re-layouts: 101 us -> none  [the longest x64 81 us: shards(): sent, meta = lax.map(outgoing, slots)]
    pallas_call x0 -> x5, Pallas kernels: none -> 90.5 us  [the longest x2 54.3 us: exchange(): pl.pallas_call(exchange_kernel, out_shape=jax.ShapeDtypeStruct(x.shape, x...]
    all_to_all x3 -> x0, waiting for transfers between devices: 56.4 us -> none  [the longest x1 27.7 us: shards(): lax.all_to_all(sent, 'tile', split_axis=0, concat_axis=0, tiled=True)]
    concatenate x130 -> x0, other arithmetic: 52 us -> none  [the longest x128 50.6 us: outgoing(): meta = jnp.concatenate([places, size_entry[None]]).astype(jnp.bfloat16)]
  transfers between devices with their start and end apart: 5 -> 2, of which waited for: 5 -> 2; matrix products, arithmetic and copies ran while one was open for 1% -> 0% of each run, Pallas kernels for 0% -> 0%
where the time goes in v1:
time: 110 us
  Pallas kernels  90.5 us (82%)
  starting transfers between devices  10.7 us (10%)
  waiting for transfers between devices  5.75 us (5%)
  local copies, waits for them, and re-layouts  2.03 us (2%)
    pallas_call x2, Pallas kernels, exchange(): pl.pallas_call(exchange_kernel, out_shape=jax.ShapeDtypeStruct(x.shape, x...  54.3 us
    pallas_call x1, Pallas kernels, shards(): pl.pallas_call(restore_kernel, grid=(CAP,), out_shape=(jax.ShapeDtypeStru...  25.1 us
    ppermute x1, starting transfers between devices, shards(): below = lax.ppermute(features[:, 0], 'tile', [(j, i) for i, j in ring])  8.75 us
    pallas_call x1, Pallas kernels, shards(): pl.pallas_call(decode_kernel, out_shape=(jax.ShapeDtypeStruct(features.sh...  7.2 us
    ppermute x1, waiting for transfers between devices, shards(): above = lax.ppermute(features[:, 1], 'tile', ring)  5.43 us
    pallas_call x1, Pallas kernels, shards(): pl.pallas_call(paste_kernel, out_shape=jax.ShapeDtypeStruct(features.shap...  3.89 us
  transfers between devices with their start and end apart: 2, of which 2 were waited for; matrix products, arithmetic and copies ran while one was open for 0% of the time, Pallas kernels for 0%

profile of v1, /device:TPU:1, one launch (start us, length us, event | category | flops | bytes accessed | tf_op | source)
XLA Modules:
  0.0 109.6 jit_solution(10661575242712867840)
XLA Ops:
  0.6 1.2 %slice_bitcast_fusion = (bf16[6,320,128]{2,1,0:T(8,128)(2,1)S(1)}, bf16[6,320,128]{2,1,0:T(8,128)(2,1)S(1)}) fusion(bf16[6,2,320,128]{3,2,1,0:T(8,128)(2,1)} %feat.1), kind=kLoop, calls=%fused_computation | loop fusion | bytes 1966080 | tf_op jit(solution)/shard_map/squeeze | solution.py:316
  1.9 8.7 %collective-permute-start.1 = (bf16[6,320,128]{2,1,0:T(8,128)(2,1)S(1)}, bf16[6,320,128]{2,1,0:T(8,128)(2,1)S(1)}, u32[]{:S(2)}, u32[]{:S(2)}) collective-permute-start(bf16[6,320,128]{2,1,0:T(8,128)(2,1)S(1)} %get-tuple-element.10), channel_id=1, source_target_pairs={{1,0},{2,1},{3,2},{4,3},{5,4},{6,5},{7,6},{8,7},{9,8},{10,9},{11,1... | collective-permute-start | bytes 1474568 | tf_op jit(solution)/shard_map/ppermute | solution.py:316
  10.6 1.9 %collective-permute-start = (bf16[6,320,128]{2,1,0:T(8,128)(2,1)S(1)}, bf16[6,320,128]{2,1,0:T(8,128)(2,1)S(1)}, u32[]{:S(2)}, u32[]{:S(2)}) collective-permute-start(bf16[6,320,128]{2,1,0:T(8,128)(2,1)S(1)} %get-tuple-element.11), channel_id=1, source_target_pairs={{0,1},{1,2},{2,3},{3,4},{4,5},{5,6},{6,7},{7,8},{8,9},{9,10},{10,1... | collective-permute-start | bytes 1474568 | tf_op jit(solution)/shard_map/ppermute | solution.py:315
  12.6 0.3 collective-permute-done.1.below
  12.9 0.0 copy-start
  12.9 5.4 %collective-permute-done.above = bf16[6,320,128]{2,1,0:T(8,128)(2,1)S(1)} collective-permute-done((bf16[6,320,128]{2,1,0:T(8,128)(2,1)S(1)}, bf16[6,320,128]{2,1,0:T(8,128)(2,1)S(1)}, u32[]{:S(2)}, u32[]{:S(2)}) %collective-permute-start) | collective-permute-done | bytes 491552 | tf_op jit(solution)/shard_map/ppermute | solution.py:315
  18.3 0.0 copy-start.1
  18.3 0.0 copy-done
  18.3 0.8 copy-done.1
  19.1 7.2 %decode.1 = (bf16[6,2,320,128]{3,2,1,0:T(8,128)(2,1)}, bf16[64,2,48,128]{3,2,1,0:T(8,128)(2,1)}) custom-call(s32[3,32]{1,0:T(4,128)} %boxes.5, s32[64]{0:T(128)} %slots.5, bf16[6,2,320,128]{3,2,1,0:T(8,128)(2,1)} %feat.1, bf16[6,320,128]{2,1,0:T(8,128)(2,1)} %copy-done.1, bf16[6,320,128]{2,1,0:T(8,128)(2,1)} %copy-done, bf16[9,128,128]{2,1,0:T(8,128)(2,1)} %w_ref.1, ...), custom_call_target="tpu_custom_call" | custom-call | tf_op jit(solution)/shard_map/decode/pallas_call | solution.py:322
  26.3 28.7 %exchange_0.1.got = bf16[32,2,2,48,128]{4,3,2,1,0:T(8,128)(2,1)} custom-call(bf16[32,2,2,48,128]{4,3,2,1,0:T(8,128)(2,1)} %bitcast.14), custom_call_target="tpu_custom_call" | custom-call | tf_op jit(solution)/shard_map/exchange_0/pallas_call | solution.py:134
  55.0 25.1 %restore.1 = (bf16[2,64,64,128]{3,2,1,0:T(8,128)(2,1)}, bf16[32,2,2,48,128]{4,3,2,1,0:T(8,128)(2,1)}) custom-call(s32[3,32]{1,0:T(4,128)} %boxes.5, s32[64]{0:T(128)} %slots.5, bf16[32,2,2,48,128]{4,3,2,1,0:T(8,128)(2,1)} %exchange_0.1.got, bf16[9,128,128]{2,1,0:T(8,128)(2,1)} %w1.1, f32[1,128]{1,0:T(1,128)} %bitcast.16, bf16[9,128,128]{2,1,0:T(8,128)(2,1)} %w2.1, ...), custom_call_target="tpu_custom_call" | custom-call | tf_op jit(solution)/shard_map/restore/pallas_call | solution.py:344
  80.1 25.6 %exchange_1.1 = bf16[32,2,2,48,128]{4,3,2,1,0:T(8,128)(2,1)} custom-call(bf16[32,2,2,48,128]{4,3,2,1,0:T(8,128)(2,1)} %get-tuple-element.8.src), custom_call_target="tpu_custom_call" | custom-call | tf_op jit(solution)/shard_map/exchange_1/pallas_call | solution.py:134
  105.7 3.9 %paste.1 = bf16[6,2,320,128]{3,2,1,0:T(8,128)(2,1)} custom-call(s32[3,32]{1,0:T(4,128)} %boxes.5, s32[64]{0:T(128)} %slots.5, bf16[6,2,320,128]{3,2,1,0:T(8,128)(2,1)} %get-tuple-element.6.dec, bf16[64,2,48,128]{3,2,1,0:T(8,128)(2,1)} %bitcast.13), custom_call_target="tpu_custom_call" | custom-call | tf_op jit(solution)/shard_map/paste/pallas_call | solution.py:378
Async XLA Ops:
  1.9 11.0 %collective-permute-start.1 = (bf16[6,320,128]{2,1,0:T(8,128)(2,1)S(1)}, bf16[6,320,128]{2,1,0:T(8,128)(2,1)S(1)}, u32[]{:S(2)}, u32[]{:S(2)}) collective-permute-start(bf16[6,320,128]{2,1,0:T(8,128)(2,1)S(1)} %get-tuple-element.10), channel_id=1, source_target_pairs={{1,0},{2,1},{3,2},{4,3},{5,4},{6,5},{7,6},{8,7},{9,8},{10,9},{11,1... | collective-permute-start | bytes 1474568 | tf_op jit(solution)/shard_map/ppermute | solution.py:316
  10.6 7.7 %collective-permute-start = (bf16[6,320,128]{2,1,0:T(8,128)(2,1)S(1)}, bf16[6,320,128]{2,1,0:T(8,128)(2,1)S(1)}, u32[]{:S(2)}, u32[]{:S(2)}) collective-permute-start(bf16[6,320,128]{2,1,0:T(8,128)(2,1)S(1)} %get-tuple-element.11), channel_id=1, source_target_pairs={{0,1},{1,2},{2,3},{3,4},{4,5},{5,6},{6,7},{7,8},{8,9},{9,10},{10,1... | collective-permute-start | bytes 1474568 | tf_op jit(solution)/shard_map/ppermute | solution.py:315
  12.9 5.4 %copy-start = (bf16[6,320,128]{2,1,0:T(8,128)(2,1)}, bf16[6,320,128]{2,1,0:T(8,128)(2,1)S(1)}, u32[]{:S(2)}) copy-start(bf16[6,320,128]{2,1,0:T(8,128)(2,1)S(1)} %collective-permute-done.1.below) | copy-start | bytes 1474564
  18.3 0.8 copy-start.1

commit v2 on v0

v2 whole, which is shorter than its diff:
```python
import jax
import jax.numpy as jnp
from jax import lax
from jax.experimental import pallas as pl
from jax.experimental.pallas import tpu as pltpu
from jax.sharding import PartitionSpec as P

S = 64
UNIT = 12
SPAN = 48
C = 128
BANDS = 6
COLS = 320
STRIDE = 64
TILES = 32
CAP = 2
FRAME = BANDS * STRIDE
SENT = 56
MESH = pl.DeviceIdType.MESH
BF = jnp.bfloat16
F32 = jnp.float32
CHUNK = 4
VMEM_LIMIT = 60 * 1024 * 1024

OFFSETS = sorted(
    [(dy, dx, dc) for dy in range(4) for dx in range(4) for dc in range(2) if dy + dx + dc],
    key=lambda d: -(min(d[0], 4 - d[0]) + min(d[1], 4 - d[1])),
)
PEERS = len(OFFSETS)


def silu(v):
    return v * (1.0 / (1.0 + jnp.exp(-v)))


def rounded(v):
    return v.astype(BF).astype(F32)


def pair_weight(w_ref, out_ref):
    zero = jnp.zeros((C, C), BF)
    for a in range(4):
        for dx in range(3):
            rows = pl.ds((a * 3 + dx) * C, C)
            out_ref[rows, 0:C] = w_ref[3 * a + dx] if a < 3 else zero
            out_ref[rows, C : 2 * C] = w_ref[3 * (a - 1) + dx] if a > 0 else zero


def widen(pad_ref, index, start, cols):
    return jnp.concatenate(
        [pad_ref[index, pl.ds(start + dx, cols), :].astype(BF) for dx in range(3)], axis=-1
    )


def conv_pairs(wide, w_pair, bias, m0, cols):
    lhs = jnp.concatenate(
        [
            wide[pl.ds(m0 + a // 2, CHUNK), a % 2].reshape(CHUNK * cols, 3 * C)
            for a in range(4)
        ],
        axis=-1,
    )
    return jnp.dot(lhs, w_pair[...], preferred_element_type=F32) + bias


def twice(b_ref):
    return jnp.concatenate([b_ref[...], b_ref[...]], axis=-1)


def main_kernel(
    boxes,
    slots,
    feat,
    w0,
    b0,
    w1,
    b1,
    w2,
    b2,
    dec_out,
    rest_out,
    back,
    w0_pair,
    w1_pair,
    w2_pair,
    fpad,
    payload,
    got,
    reg,
    wide0,
    cut,
    pad,
    pad2,
    wide,
    wide2,
    delta,
    rest,
    ret,
    halo,
    hpad,
    dwide,
    dec,
    fwd_send,
    fwd_recv,
    ret_send,
    ret_recv,
    halo_send,
    halo_recv,
    local_sem,
):
    me = lax.axis_index("tile")
    y, x, core = me // 8, (me // 2) % 4, me % 2
    targets = [
        ((y + dy) % 4) * 8 + ((x + dx) % 4) * 2 + (core + dc) % 2 for dy, dx, dc in OFFSETS
    ]
    barrier = pltpu.get_barrier_semaphore()
    for t in targets:
        pl.semaphore_signal(barrier, inc=1, device_id={"tile": t}, device_id_type=MESH)

    def remote(src, dst, send, recv, t):
        return pltpu.make_async_remote_copy(
            src_ref=src,
            dst_ref=dst,
            send_sem=send,
            recv_sem=recv,
            device_id={"tile": t},
            device_id_type=MESH,
        )

    def forward(s):
        return [
            remote(
                payload.at[s, t], got.at[s, me], fwd_send.at[s, k], fwd_recv.at[s, k], t
            )
            for k, t in enumerate(targets)
        ]

    def backward(s):
        return [
            remote(ret.at[s, t], back.at[s, me], ret_send.at[s, k], ret_recv.at[s, k], t)
            for k, t in enumerate(targets)
        ]

    def own_forward(s):
        return pltpu.make_async_copy(payload.at[s, me], got.at[s, me], local_sem.at[s])

    def own_backward(s):
        return pltpu.make_async_copy(ret.at[s, me], back.at[s, me], local_sem.at[2 + s])

    def keep_rest(s):
        return pltpu.make_async_copy(rest.at[s], rest_out.at[s], local_sem.at[4 + s])

    def rims():
        after, ahead = (me + 1) % TILES, (me + TILES - 1) % TILES
        return [
            remote(feat.at[:, 1], halo.at[0], halo_send.at[0], halo_recv.at[0], after),
            remote(feat.at[:, 0], halo.at[1], halo_send.at[1], halo_recv.at[1], ahead),
        ]

    fpad[:, 0:8, :] = jnp.zeros((2 * BANDS, 8, C), F32)
    fpad[:, COLS + 8 : COLS + 16, :] = jnp.zeros((2 * BANDS, 8, C), F32)
    for b in range(BANDS):
        for o in range(2):
            fpad[2 * b + o, 8 : COLS + 8, :] = feat[b, o].astype(F32)

    def fill(s):
        def body(w, _):
            crop = jnp.maximum(slots[CAP * w + s], 0)
            row0 = boxes[0, crop] - 1
            col0 = boxes[1, crop]
            parts = []
            for i in range(2):
                h = (2 * me + i - row0) & (STRIDE - 1)
                band = jnp.clip((row0 + h) >> 6, 0, BANDS - 1)
                parts.append(fpad[2 * band + i, pl.ds(col0 + 7, SENT), :])
            payload[s, w] = jnp.concatenate(parts, axis=0).astype(BF)
            return 0

        lax.fori_loop(0, TILES, body, 0, unroll=2)

    fill(0)
    pl.semaphore_wait(barrier, PEERS)
    for copy in forward(0):
        copy.start()
    own_forward(0).start()
    fill(1)
    for copy in forward(1):
        copy.start()
    own_forward(1).start()
    for copy in rims():
        copy.start()

    pair_weight(w0, w0_pair)
    pair_weight(w1, w1_pair)
    pair_weight(w2, w2_pair)
    for ref in (pad, pad2):
        ref[:, 0:8, :] = jnp.zeros((S, 8, C), F32)
        ref[:, S + 8 : S + 16, :] = jnp.zeros((S, 8, C), F32)
    for ref in (wide, wide2):
        ref[0, 0] = jnp.zeros((S, 3 * C), BF)
        ref[S // 2, 1] = jnp.zeros((S, 3 * C), BF)
    reg[STRIDE] = jnp.zeros((SENT, C), F32)
    hpad[:, 0:8, :] = jnp.zeros((2, 8, C), F32)
    hpad[:, COLS + 8 : COLS + 16, :] = jnp.zeros((2, 8, C), F32)
    bias0, bias1, bias2 = twice(b0), twice(b1), twice(b2)

    def restore(s, _):
        own_forward(s).wait()
        for copy in forward(s):
            copy.wait_recv()
        slot = slots[CAP * me + s]
        crop = jnp.maximum(slot, 0)
        row0 = boxes[0, crop]
        side = UNIT * (boxes[2, crop] + 2)
        sidef = side.astype(F32)

        def unpack(p, _):
            block = got[s, p].astype(F32)
            reg[2 * p] = block[0:SENT]
            reg[2 * p + 1] = block[SENT : 2 * SENT]
            return 0

        lax.fori_loop(0, TILES, unpack, 0, unroll=4)

        def region(h, _):
            for o in range(2):
                row = row0 - 1 + 2 * h + o
                live = (row >= 0) & (row < FRAME)
                index = jnp.where(live, row & (STRIDE - 1), STRIDE)
                wide0[h, o] = widen(reg, index, 0, SPAN)
            return 0

        lax.fori_loop(0, SPAN // 2 + 1, region, 0)

        spot = (lax.broadcasted_iota(jnp.int32, (S, SPAN), 0).astype(F32) + 0.5) * sidef / S
        spot = jnp.clip(spot - 0.5, 0.0, sidef - 1.0)
        cell = lax.broadcasted_iota(jnp.int32, (S, SPAN), 1).astype(F32)
        down = jnp.maximum(0.0, 1.0 - jnp.abs(spot - cell)).astype(BF)

        def decode(j, _):
            m0 = j * CHUNK
            act = silu(conv_pairs(wide0, w0_pair, bias0, m0, SPAN))
            act = act.reshape(CHUNK, SPAN, 2 * C)
            for i in range(CHUNK):
                centre = jnp.concatenate(
                    [wide0[m0 + i, 1, :, C : 2 * C], wide0[m0 + i + 1, 0, :, C : 2 * C]], axis=-1
                )
                value = (centre.astype(F32) + act[i]).astype(BF)
                z = rounded(jnp.dot(down, value, preferred_element_type=F32))
                cut[2 * (m0 + i)] = z[:, 0:C]
                cut[2 * (m0 + i) + 1] = z[:, C : 2 * C]
            return 0

        lax.fori_loop(0, SPAN // 2 // CHUNK, decode, 0)

        def spread(source, target, group):
            for k in range(2 * CHUNK):
                row = group * 2 * CHUNK + k
                target[(row + 1) >> 1, (row + 1) & 1] = widen(source, row, 7, S)

        def crop_rows(g, _):
            spread(pad, wide, jnp.maximum(g - 1, 0))
            for k in range(2 * CHUNK):
                t = g * 2 * CHUNK + k
                num = jnp.clip((2 * t + 1) * side - S, 0, (side - 1) * 128)
                first = num >> 7
                second = jnp.minimum(first + 1, SPAN - 1)
                frac = (num & 127).astype(F32) * (1.0 / 128.0)
                pad[t, 8 : S + 8, :] = rounded((1.0 - frac) * cut[first] + frac * cut[second])
            return 0

        groups = S // (2 * CHUNK)
        lax.fori_loop(0, groups, crop_rows, 0)
        spread(pad, wide, groups - 1)

        def first_conv(j, _):
            spread(pad2, wide2, jnp.maximum(j - 1, 0))
            v = rounded(silu(conv_pairs(wide, w1_pair, bias1, j * CHUNK, S)))
            v = v.reshape(CHUNK, S, 2 * C)
            for i in range(CHUNK):
                for o in range(2):
                    pad2[2 * (j * CHUNK + i) + o, 8 : S + 8, :] = v[i, :, o * C : (o + 1) * C]
            return 0

        lax.fori_loop(0, groups, first_conv, 0)
        spread(pad2, wide2, groups - 1)
        keep = slot >= 0

        def second_conv(j, _):
            v = rounded(conv_pairs(wide2, w2_pair, bias2, j * CHUNK, S))
            v = v.reshape(CHUNK, S, 2 * C)
            for i in range(CHUNK):
                for o in range(2):
                    row = 2 * (j * CHUNK + i) + o
                    part = v[i, :, o * C : (o + 1) * C]
                    delta[row] = part
                    rest[s, row] = jnp.where(keep, part, 0.0).astype(BF)
            return 0

        lax.fori_loop(0, groups, second_conv, 0)
        keep_rest(s).start()

        where = (lax.broadcasted_iota(jnp.int32, (SPAN, S), 0).astype(F32) + 0.5) * S / sidef
        where = jnp.clip(where - 0.5, 0.0, S - 1.0)
        inside = lax.broadcasted_iota(jnp.int32, (SPAN, S), 0) < side
        grid = lax.broadcasted_iota(jnp.int32, (SPAN, S), 1).astype(F32)
        lift = jnp.where(inside, jnp.maximum(0.0, 1.0 - jnp.abs(where - grid)), 0.0)
        lift_high = lift.astype(BF)
        lift_low = (lift - lift_high.astype(F32)).astype(BF)
        lifts = jnp.concatenate([lift_high, lift_low], axis=-1)
        magic = jnp.where(side == 24, 10923, jnp.where(side == 36, 7282, 5462))
        inverse = jnp.where(side == 24, 1.0 / 24, jnp.where(side == 36, 1.0 / 36, 1.0 / 48))

        def patch(p, _):
            halves = []
            for i in range(2):
                h = (2 * p + i - row0) & (STRIDE - 1)
                num = jnp.clip((2 * h + 1) * (S // 2) - (side >> 1), 0, (S - 1) * side)
                one = (num * magic) >> 18
                frac = (num - one * side).astype(F32) * inverse
                live = (h < side).astype(F32)
                two = jnp.minimum(one + 1, S - 1)
                halves.append(
                    ((live - live * frac) * delta[one] + (live * frac) * delta[two]).astype(BF)
                )
            rhs = jnp.concatenate(halves, axis=-1)
            rhs = jnp.concatenate([rhs, rhs], axis=0)
            z = jnp.dot(lifts, rhs, preferred_element_type=F32).astype(BF)
            ret[s, p, 0] = z[:, 0:C]
            ret[s, p, 1] = z[:, C : 2 * C]
            return 0

        lax.fori_loop(0, TILES, patch, 0, unroll=4)
        for copy in backward(s):
            copy.start()
        own_backward(s).start()
        return 0

    lax.fori_loop(0, CAP, restore, 0)

    for copy in rims():
        copy.wait_recv()

    def band(b, _):
        up = jnp.where(me == 0, b - 1, b)
        low = jnp.where(me == TILES - 1, b + 1, b)
        up_ok = (up >= 0).astype(F32)
        low_ok = (low < BANDS).astype(F32)
        hpad[0, 8 : COLS + 8, :] = halo[0, jnp.maximum(up, 0)].astype(F32) * up_ok
        hpad[1, 8 : COLS + 8, :] = halo[1, jnp.minimum(low, BANDS - 1)].astype(F32) * low_ok
        dwide[0] = widen(hpad, 0, 7, COLS)
        dwide[1] = widen(fpad, 2 * b, 7, COLS)
        dwide[2] = widen(fpad, 2 * b + 1, 7, COLS)
        dwide[3] = widen(hpad, 1, 7, COLS)
        for part in range(2):
            rows = pl.ds(part * (COLS // 2), COLS // 2)
            lhs = jnp.concatenate([dwide[a, rows, :] for a in range(4)], axis=-1)
            act = silu(jnp.dot(lhs, w0_pair[...], preferred_element_type=F32) + bias0)
            for o in range(2):
                v = feat[b, o, rows, :].astype(F32) + act[:, o * C : (o + 1) * C]
                dec[b, o, rows, :] = v.astype(BF)
        return 0

    lax.fori_loop(0, BANDS, band, 0)
    out = pltpu.make_async_copy(dec, dec_out, local_sem.at[6])
    out.start()
    for copy in rims():
        copy.wait_send()
    for s in range(CAP):
        for copy in forward(s):
            copy.wait_send()
        keep_rest(s).wait()
        own_backward(s).wait()
    for s in range(CAP):
        for copy in backward(s):
            copy.wait()
    out.wait()


def paste_kernel(boxes, slots, dec, back, rest_in, out, rest_out, acc, held, sem):
    position = lax.axis_index("tile")
    fetch = pltpu.make_async_copy(rest_in, held, sem.at[0])
    fetch.start()
    for b in range(BANDS):
        for o in range(2):
            acc[2 * b + o] = dec[b, o].astype(F32)
    fetch.wait()
    store = pltpu.make_async_copy(held, rest_out, sem.at[1])
    store.start()

    for s in range(CAP):

        def body(w, _):
            slot = slots[CAP * w + s]
            crop = jnp.maximum(slot, 0)
            row0 = boxes[0, crop]
            cols = pl.ds(boxes[1, crop], SPAN)
            for i in range(2):
                h = (2 * position + i - row0) & (STRIDE - 1)
                live = (slot >= 0) & (h < SPAN)
                row = jnp.where(live, 2 * ((row0 + h) >> 6) + i, 2 * BANDS + i)
                acc[row, cols, :] = acc[row, cols, :] + back[s, w, i].astype(F32)
            return 0

        lax.fori_loop(0, TILES, body, 0, unroll=2)
    for b in range(BANDS):
        for o in range(2):
            out[b, o] = acc[2 * b + o].astype(BF)
    store.wait()


def shards(
    features,
    dec_weight,
    dec_bias,
    first_weight,
    first_bias,
    second_weight,
    second_bias,
    boxes,
    slots,
):
    smem = pl.BlockSpec(memory_space=pltpu.SMEM)
    vmem = pl.BlockSpec(memory_space=pltpu.VMEM)
    any_ = pl.BlockSpec(memory_space=pl.ANY)
    rest_type = jax.ShapeDtypeStruct((CAP, S, S, C), BF)
    frame_type = jax.ShapeDtypeStruct(features.shape, BF)
    dma = pltpu.SemaphoreType.DMA
    pair = pltpu.VMEM((12 * C, 2 * C), BF)
    padded = pltpu.VMEM((S, S + 16, C), F32)
    spread = pltpu.VMEM((S // 2 + 1, 2, S, 3 * C), BF)
    sent = pltpu.VMEM((CAP, TILES, 2 * SENT, C), BF)

    decoded, rest, back = pl.pallas_call(
        main_kernel,
        out_shape=(
            frame_type,
            rest_type,
            jax.ShapeDtypeStruct((CAP, TILES, 2, SPAN, C), BF),
        ),
        in_specs=[smem, smem] + [vmem] * 7,
        out_specs=(any_, any_, any_),
        scratch_shapes=[
            pair,
            pair,
            pair,
            pltpu.VMEM((2 * BANDS, COLS + 16, C), F32),
            sent,
            sent,
            pltpu.VMEM((STRIDE + 1, SENT, C), F32),
            pltpu.VMEM((SPAN // 2 + 1, 2, SPAN, 3 * C), BF),
            pltpu.VMEM((SPAN, S, C), F32),
            padded,
            padded,
            spread,
            spread,
            pltpu.VMEM((S, S, C), F32),
            pltpu.VMEM((CAP, S, S, C), BF),
            pltpu.VMEM((CAP, TILES, 2, SPAN, C), BF),
            pltpu.VMEM((2, BANDS, COLS, C), BF),
            pltpu.VMEM((2, COLS + 16, C), F32),
            pltpu.VMEM((4, COLS, 3 * C), BF),
            pltpu.VMEM((BANDS, 2, COLS, C), BF),
            dma((CAP, PEERS)),
            dma((CAP, PEERS)),
            dma((CAP, PEERS)),
            dma((CAP, PEERS)),
            dma((2,)),
            dma((2,)),
            dma((7,)),
        ],
        compiler_params=pltpu.CompilerParams(
            collective_id=0, has_side_effects=True, vmem_limit_bytes=VMEM_LIMIT
        ),
        name="main",
    )(
        boxes,
        slots,
        features,
        dec_weight,
        dec_bias[None],
        first_weight,
        first_bias[None],
        second_weight,
        second_bias[None],
    )

    return pl.pallas_call(
        paste_kernel,
        out_shape=(frame_type, rest_type),
        in_specs=[smem, smem, vmem, vmem, any_],
        out_specs=(vmem, any_),
        scratch_shapes=[
            pltpu.VMEM((2 * BANDS + 2, COLS, C), F32),
            pltpu.VMEM((CAP, S, S, C), BF),
            dma((2,)),
        ],
        compiler_params=pltpu.CompilerParams(vmem_limit_bytes=VMEM_LIMIT),
        name="paste",
    )(boxes, slots, decoded, back, rest)


def solution(mesh):
    return jax.shard_map(
        shards,
        mesh=mesh,
        in_specs=(
            P("sess", "tile", None, None),
            P(),
            P(),
            P(),
            P(),
            P(),
            P(),
            P(None, "sess"),
            P("sess"),
        ),
        out_specs=(P("sess", "tile", None, None), P(("sess", "tile"), None, None, None)),
        check_vma=False,
    )
```

time: 1450 us -> 74 us (0.05); the launches traced: 1430 us -> 73.8 us
  loops' own time: 710 us -> 0 us
  local copies, waits for them, and re-layouts: 293 us -> 0 us
  other arithmetic: 231 us -> 0 us
  matrix products: 107 us -> 0 us
  Pallas kernels: 0 us -> 73.2 us
  waiting for transfers between devices: 62.2 us -> 0 us
  starting transfers between devices: 30.7 us -> 0 us
    another operation x3 -> x0, loops' own time: 710 us -> none  [the longest x1 382 us: shards(): sent, meta = lax.map(outgoing, slots)]
    reduce_sum x128 -> x0, other arithmetic: 161 us -> none  [locate(): start = jnp.sum((global_rows < row0).astype(jnp.int32))]
    dynamic_slice x260 -> x0, local copies, waits for them, and re-layouts: 161 us -> none  [the longest x128 84.9 us: locate(): length = UNIT * (boxes[2, crop] + 2)]
    dot_general x145 -> x0, matrix products: 107 us -> none  [the longest x64 63.5 us: paste_slot(): jnp.einsum('wt,rtc->rwc', lift, incoming.astype(jnp.float32), precision=h...]
    dynamic_update_slice x128 -> x0, local copies, waits for them, and re-layouts: 101 us -> none  [the longest x64 81 us: shards(): sent, meta = lax.map(outgoing, slots)]
    pallas_call x0 -> x2, Pallas kernels: none -> 73.2 us  [the longest x1 67.6 us: shards(): pl.pallas_call(main_kernel, out_shape=(frame_type, rest_type, jax.ShapeDt...]
    all_to_all x3 -> x0, waiting for transfers between devices: 56.4 us -> none  [the longest x1 27.7 us: shards(): lax.all_to_all(sent, 'tile', split_axis=0, concat_axis=0, tiled=True)]
    concatenate x130 -> x0, other arithmetic: 52 us -> none  [the longest x128 50.6 us: outgoing(): meta = jnp.concatenate([places, size_entry[None]]).astype(jnp.bfloat16)]
  transfers between devices with their start and end apart: 5 -> 0, of which waited for: 5 -> 0; matrix products, arithmetic and copies ran while one was open for 1% -> 0% of each run, Pallas kernels for 0% -> 0%
where the time goes in v2:
time: 74 us; the launch traced here: 73.8 us
  Pallas kernels  73.2 us (99%)
    pallas_call x1, Pallas kernels, shards(): pl.pallas_call(main_kernel, out_shape=(frame_type, rest_type, jax.ShapeDt...  67.6 us
    pallas_call x1, Pallas kernels, shards(): pl.pallas_call(paste_kernel, out_shape=(frame_type, rest_type), in_specs=...  5.59 us

profile of v2, /device:TPU:1, one launch (start us, length us, event | category | flops | bytes accessed | tf_op | source)
XLA Modules:
  0.0 73.8 jit_solution(8360695795275796849)
XLA Ops:
  0.6 67.6 %main.1 = (bf16[6,2,320,128]{3,2,1,0:T(8,128)(2,1)}, bf16[2,64,64,128]{3,2,1,0:T(8,128)(2,1)}, bf16[2,32,2,48,128]{4,3,2,1,0:T(8,128)(2,1)}) custom-call(s32[3,32]{1,0:T(4,128)} %boxes.3, s32[64]{0:T(128)} %slots.3, bf16[6,2,320,128]{3,2,1,0:T(8,128)(2,1)} %feat.1, bf16[9,128,128]{2,1,0:T(8,128)(2,1)} %w0.1, f32[1,128]{1,0:T(1,128)} %bitcast.3, ...), custom_call_target="tpu_custom_call" | custom-call | tf_op jit(solution)/shard_map/main/pallas_call | solution.py:434
  68.2 5.6 %paste.1 = (bf16[6,2,320,128]{3,2,1,0:T(8,128)(2,1)}, bf16[2,64,64,128]{3,2,1,0:T(8,128)(2,1)}) custom-call(s32[3,32]{1,0:T(4,128)} %boxes.3, s32[64]{0:T(128)} %slots.3, bf16[6,2,320,128]{3,2,1,0:T(8,128)(2,1)} %get-tuple-element.5.dec, bf16[2,32,2,48,128]{4,3,2,1,0:T(8,128)(2,1)} %get-tuple-element.6.back, bf16[2,64,64,128]{3,2,1,0:T(8,128)(2,1)} %get-tuple-element.7.rest_in), custom_call_target="tpu_custom_call" | custom-call | tf_op jit(solution)/shard_map/paste/pallas_call | solution.py:488

commit v3 on v2

--- a/solution.py
+++ b/solution.py
@@ -20,6 +20,10 @@
 BF = jnp.bfloat16
 F32 = jnp.float32
 CHUNK = 4
+U_DEC = 3
+U_CONV1 = 2
+U_CONV2 = 2
+U_PATCH = 8
 VMEM_LIMIT = 60 * 1024 * 1024
 
 OFFSETS = sorted(
@@ -30,7 +34,8 @@
 
 
 def silu(v):
-    return v * (1.0 / (1.0 + jnp.exp(-v)))
+    half = 0.5 * v
+    return half + half * jnp.tanh(half)
 
 
 def rounded(v):
@@ -50,6 +55,15 @@
     return jnp.concatenate(
         [pad_ref[index, pl.ds(start + dx, cols), :].astype(BF) for dx in range(3)], axis=-1
     )
+
+
+def spread_row(v):
+    cell = lax.broadcasted_iota(jnp.int32, (8, C), 0)
+    left = pltpu.roll(v, 1, 0)
+    left = jnp.concatenate([jnp.where(cell == 0, 0.0, left[0:8]), left[8:]], axis=0)
+    right = pltpu.roll(v, S - 1, 0)
+    right = jnp.concatenate([right[: S - 8], jnp.where(cell == 7, 0.0, right[S - 8 :])], axis=0)
+    return jnp.concatenate([left.astype(BF), v.astype(BF), right.astype(BF)], axis=-1)
 
 
 def conv_pairs(wide, w_pair, bias, m0, cols):
@@ -88,9 +102,8 @@
     got,
     reg,
     wide0,
+    value,
     cut,
-    pad,
-    pad2,
     wide,
     wide2,
     delta,
@@ -193,9 +206,6 @@
     pair_weight(w0, w0_pair)
     pair_weight(w1, w1_pair)
     pair_weight(w2, w2_pair)
-    for ref in (pad, pad2):
-        ref[:, 0:8, :] = jnp.zeros((S, 8, C), F32)
-        ref[:, S + 8 : S + 16, :] = jnp.zeros((S, 8, C), F32)
     for ref in (wide, wide2):
         ref[0, 0] = jnp.zeros((S, 3 * C), BF)
         ref[S // 2, 1] = jnp.zeros((S, 3 * C), BF)
@@ -220,7 +230,7 @@
             reg[2 * p + 1] = block[SENT : 2 * SENT]
             return 0
 
-        lax.fori_loop(0, TILES, unpack, 0, unroll=4)
+        lax.fori_loop(0, TILES, unpack, 0, unroll=8)
 
         def region(h, _):
             for o in range(2):
@@ -230,7 +240,7 @@
                 wide0[h, o] = widen(reg, index, 0, SPAN)
             return 0
 
-        lax.fori_loop(0, SPAN // 2 + 1, region, 0)
+        lax.fori_loop(0, SPAN // 2 + 1, region, 0, unroll=5)
 
         spot = (lax.broadcasted_iota(jnp.int32, (S, SPAN), 0).astype(F32) + 0.5) * sidef / S
         spot = jnp.clip(spot - 0.5, 0.0, sidef - 1.0)
@@ -245,45 +255,40 @@
                 centre = jnp.concatenate(
                     [wide0[m0 + i, 1, :, C : 2 * C], wide0[m0 + i + 1, 0, :, C : 2 * C]], axis=-1
                 )
-                value = (centre.astype(F32) + act[i]).astype(BF)
-                z = rounded(jnp.dot(down, value, preferred_element_type=F32))
-                cut[2 * (m0 + i)] = z[:, 0:C]
-                cut[2 * (m0 + i) + 1] = z[:, C : 2 * C]
-            return 0
-
-        lax.fori_loop(0, SPAN // 2 // CHUNK, decode, 0)
-
-        def spread(source, target, group):
-            for k in range(2 * CHUNK):
-                row = group * 2 * CHUNK + k
-                target[(row + 1) >> 1, (row + 1) & 1] = widen(source, row, 7, S)
-
-        def crop_rows(g, _):
-            spread(pad, wide, jnp.maximum(g - 1, 0))
-            for k in range(2 * CHUNK):
-                t = g * 2 * CHUNK + k
-                num = jnp.clip((2 * t + 1) * side - S, 0, (side - 1) * 128)
-                first = num >> 7
-                second = jnp.minimum(first + 1, SPAN - 1)
-                frac = (num & 127).astype(F32) * (1.0 / 128.0)
-                pad[t, 8 : S + 8, :] = rounded((1.0 - frac) * cut[first] + frac * cut[second])
-            return 0
-
+                value[m0 + i] = (centre.astype(F32) + act[i]).astype(BF)
+            return 0
+
+        lax.fori_loop(0, SPAN // 2 // CHUNK, decode, 0, unroll=U_DEC)
+
+        def colcut(m, _):
+            z = rounded(jnp.dot(down, value[m], preferred_element_type=F32))
+            cut[2 * m] = z[:, 0:C]
+            cut[2 * m + 1] = z[:, C : 2 * C]
+            return 0
+
+        lax.fori_loop(0, SPAN // 2, colcut, 0, unroll=12)
+
+        def crop_row(t, _):
+            num = jnp.clip((2 * t + 1) * side - S, 0, (side - 1) * 128)
+            first = num >> 7
+            second = jnp.minimum(first + 1, SPAN - 1)
+            frac = (num & 127).astype(F32) * (1.0 / 128.0)
+            v = (1.0 - frac) * cut[first] + frac * cut[second]
+            wide[(t + 1) >> 1, (t + 1) & 1] = spread_row(v)
+            return 0
+
+        lax.fori_loop(0, S, crop_row, 0, unroll=8)
         groups = S // (2 * CHUNK)
-        lax.fori_loop(0, groups, crop_rows, 0)
-        spread(pad, wide, groups - 1)
 
         def first_conv(j, _):
-            spread(pad2, wide2, jnp.maximum(j - 1, 0))
-            v = rounded(silu(conv_pairs(wide, w1_pair, bias1, j * CHUNK, S)))
+            v = silu(conv_pairs(wide, w1_pair, bias1, j * CHUNK, S))
             v = v.reshape(CHUNK, S, 2 * C)
             for i in range(CHUNK):
-                for o in range(2):
-                    pad2[2 * (j * CHUNK + i) + o, 8 : S + 8, :] = v[i, :, o * C : (o + 1) * C]
-            return 0
-
-        lax.fori_loop(0, groups, first_conv, 0)
-        spread(pad2, wide2, groups - 1)
+                wide2[j * CHUNK + i, 1] = spread_row(v[i, :, 0:C])
+                wide2[j * CHUNK + i + 1, 0] = spread_row(v[i, :, C : 2 * C])
+            return 0
+
+        lax.fori_loop(0, groups, first_conv, 0, unroll=U_CONV1)
         keep = slot >= 0
 
         def second_conv(j, _):
@@ -297,7 +302,7 @@
                     rest[s, row] = jnp.where(keep, part, 0.0).astype(BF)
             return 0
 
-        lax.fori_loop(0, groups, second_conv, 0)
+        lax.fori_loop(0, groups, second_conv, 0, unroll=U_CONV2)
         keep_rest(s).start()
 
         where = (lax.broadcasted_iota(jnp.int32, (SPAN, S), 0).astype(F32) + 0.5) * S / sidef
@@ -307,11 +312,11 @@
         lift = jnp.where(inside, jnp.maximum(0.0, 1.0 - jnp.abs(where - grid)), 0.0)
         lift_high = lift.astype(BF)
         lift_low = (lift - lift_high.astype(F32)).astype(BF)
-        lifts = jnp.concatenate([lift_high, lift_low], axis=-1)
+        lifts = jnp.concatenate([lift_high, lift_low], axis=0)
         magic = jnp.where(side == 24, 10923, jnp.where(side == 36, 7282, 5462))
         inverse = jnp.where(side == 24, 1.0 / 24, jnp.where(side == 36, 1.0 / 36, 1.0 / 48))
 
-        def patch(p, _):
+        def patch(p):
             halves = []
             for i in range(2):
                 h = (2 * p + i - row0) & (STRIDE - 1)
@@ -324,14 +329,18 @@
                     ((live - live * frac) * delta[one] + (live * frac) * delta[two]).astype(BF)
                 )
             rhs = jnp.concatenate(halves, axis=-1)
-            rhs = jnp.concatenate([rhs, rhs], axis=0)
-            z = jnp.dot(lifts, rhs, preferred_element_type=F32).astype(BF)
+            z = jnp.dot(lifts, rhs, preferred_element_type=F32)
+            z = (z[0:SPAN] + z[SPAN : 2 * SPAN]).astype(BF)
             ret[s, p, 0] = z[:, 0:C]
             ret[s, p, 1] = z[:, C : 2 * C]
-            return 0
-
-        lax.fori_loop(0, TILES, patch, 0, unroll=4)
-        for copy in backward(s):
+
+        copies = backward(s)
+        for k0 in range(0, PEERS + 1, U_PATCH):
+            for t in (targets + [me])[k0 : k0 + U_PATCH]:
+                patch(t)
+            for copy in copies[max(k0 - U_PATCH, 0) : k0]:
+                copy.start()
+        for copy in copies[PEERS + 1 - U_PATCH :]:
             copy.start()
         own_backward(s).start()
         return 0
@@ -377,36 +386,55 @@
     out.wait()
 
 
-def paste_kernel(boxes, slots, dec, back, rest_in, out, rest_out, acc, held, sem):
+def paste_kernel(
+    boxes, slots, dec_in, back_in, rest_in, out, rest_out, dec, back, rest, acc, done, sem
+):
     position = lax.axis_index("tile")
-    fetch = pltpu.make_async_copy(rest_in, held, sem.at[0])
-    fetch.start()
+    fetch_dec = pltpu.make_async_copy(dec_in, dec, sem.at[0])
+    fetch_back = [
+        pltpu.make_async_copy(back_in.at[s], back.at[s], sem.at[1 + s]) for s in range(CAP)
+    ]
+    fetch_rest = pltpu.make_async_copy(rest_in, rest, sem.at[3])
+    store_rest = pltpu.make_async_copy(rest, rest_out, sem.at[4])
+    fetch_dec.start()
+    for copy in fetch_back:
+        copy.start()
+    fetch_rest.start()
+    fetch_dec.wait()
     for b in range(BANDS):
         for o in range(2):
             acc[2 * b + o] = dec[b, o].astype(F32)
-    fetch.wait()
-    store = pltpu.make_async_copy(held, rest_out, sem.at[1])
-    store.start()
 
     for s in range(CAP):
+        fetch_back[s].wait()
 
         def body(w, _):
             slot = slots[CAP * w + s]
-            crop = jnp.maximum(slot, 0)
-            row0 = boxes[0, crop]
-            cols = pl.ds(boxes[1, crop], SPAN)
-            for i in range(2):
-                h = (2 * position + i - row0) & (STRIDE - 1)
-                live = (slot >= 0) & (h < SPAN)
-                row = jnp.where(live, 2 * ((row0 + h) >> 6) + i, 2 * BANDS + i)
-                acc[row, cols, :] = acc[row, cols, :] + back[s, w, i].astype(F32)
-            return 0
-
-        lax.fori_loop(0, TILES, body, 0, unroll=2)
+
+            @pl.when(slot >= 0)
+            def _():
+                row0 = boxes[0, slot]
+                cols = pl.ds(boxes[1, slot], SPAN)
+                for i in range(2):
+                    h = (2 * position + i - row0) & (STRIDE - 1)
+                    row = jnp.where(h < SPAN, 2 * ((row0 + h) >> 6) + i, 2 * BANDS + i)
+                    acc[row, cols, :] = acc[row, cols, :] + back[s, w, i].astype(F32)
+
+            return 0
+
+        lax.fori_loop(0, TILES, body, 0)
+        if s == 0:
+            fetch_rest.wait()
+            store_rest.start()
+    stores = []
     for b in range(BANDS):
         for o in range(2):
-            out[b, o] = acc[2 * b + o].astype(BF)
-    store.wait()
+            done[b, o] = acc[2 * b + o].astype(BF)
+        stores.append(pltpu.make_async_copy(done.at[b], out.at[b], sem.at[5 + b]))
+        stores[-1].start()
+    store_rest.wait()
+    for copy in stores:
+        copy.wait()
 
 
 def shards(
@@ -427,7 +455,6 @@
     frame_type = jax.ShapeDtypeStruct(features.shape, BF)
     dma = pltpu.SemaphoreType.DMA
     pair = pltpu.VMEM((12 * C, 2 * C), BF)
-    padded = pltpu.VMEM((S, S + 16, C), F32)
     spread = pltpu.VMEM((S // 2 + 1, 2, S, 3 * C), BF)
     sent = pltpu.VMEM((CAP, TILES, 2 * SENT, C), BF)
 
@@ -449,9 +476,8 @@
             sent,
             pltpu.VMEM((STRIDE + 1, SENT, C), F32),
             pltpu.VMEM((SPAN // 2 + 1, 2, SPAN, 3 * C), BF),
+            pltpu.VMEM((SPAN // 2, SPAN, 2 * C), BF),
             pltpu.VMEM((SPAN, S, C), F32),
-            padded,
-            padded,
             spread,
             spread,
             pltpu.VMEM((S, S, C), F32),
@@ -488,12 +514,15 @@
     return pl.pallas_call(
         paste_kernel,
         out_shape=(frame_type, rest_type),
-        in_specs=[smem, smem, vmem, vmem, any_],
-        out_specs=(vmem, any_),
+        in_specs=[smem, smem, any_, any_, any_],
+        out_specs=(any_, any_),
         scratch_shapes=[
+            pltpu.VMEM((BANDS, 2, COLS, C), BF),
+            pltpu.VMEM((CAP, TILES, 2, SPAN, C), BF),
+            pltpu.VMEM((CAP, S, S, C), BF),
             pltpu.VMEM((2 * BANDS + 2, COLS, C), F32),
-            pltpu.VMEM((CAP, S, S, C), BF),
-            dma((2,)),
+            pltpu.VMEM((BANDS, 2, COLS, C), BF),
+            dma((5 + BANDS,)),
         ],
         compiler_params=pltpu.CompilerParams(vmem_limit_bytes=VMEM_LIMIT),
         name="paste",

time: 74 us -> 65.1 us (0.88)
  Pallas kernels: 73.2 us -> 64.3 us
    pallas_call x1, Pallas kernels: 67.6 us -> 59.5 us  [shards(): pl.pallas_call(main_kernel, out_shape=(frame_type, rest_type, jax.ShapeDt...]
    pallas_call x1, Pallas kernels: 5.59 us -> 4.8 us  [shards(): pl.pallas_call(paste_kernel, out_shape=(frame_type, rest_type), in_specs=...]
where the time goes in v3:
time: 65.1 us; the launch traced here: 64.9 us
  Pallas kernels  64.3 us (99%)
    pallas_call x1, Pallas kernels, shards(): pl.pallas_call(main_kernel, out_shape=(frame_type, rest_type, jax.ShapeDt...  59.5 us
    pallas_call x1, Pallas kernels, shards(): pl.pallas_call(paste_kernel, out_shape=(frame_type, rest_type), in_specs=...  4.8 us

profile of v3, /device:TPU:1, one launch (start us, length us, event | category | flops | bytes accessed | tf_op | source)
XLA Modules:
  0.0 64.9 jit_solution(544279031385147580)
XLA Ops:
  0.6 59.5 %main.1 = (bf16[6,2,320,128]{3,2,1,0:T(8,128)(2,1)}, bf16[2,64,64,128]{3,2,1,0:T(8,128)(2,1)}, bf16[2,32,2,48,128]{4,3,2,1,0:T(8,128)(2,1)}) custom-call(s32[3,32]{1,0:T(4,128)} %boxes.3, s32[64]{0:T(128)} %slots.3, bf16[6,2,320,128]{3,2,1,0:T(8,128)(2,1)} %feat.1, bf16[9,128,128]{2,1,0:T(8,128)(2,1)} %w0.1, f32[1,128]{1,0:T(1,128)} %bitcast.3, ...), custom_call_target="tpu_custom_call" | custom-call | tf_op jit(solution)/shard_map/main/pallas_call | solution.py:461
  60.1 4.8 %paste.1 = (bf16[6,2,320,128]{3,2,1,0:T(8,128)(2,1)}, bf16[2,64,64,128]{3,2,1,0:T(8,128)(2,1)}) custom-call(s32[3,32]{1,0:T(4,128)} %boxes.3, s32[64]{0:T(128)} %slots.3, bf16[6,2,320,128]{3,2,1,0:T(8,128)(2,1)} %get-tuple-element.5.dec_in, bf16[2,32,2,48,128]{4,3,2,1,0:T(8,128)(2,1)} %get-tuple-element.6.back_in, ...), custom_call_target="tpu_custom_call" | custom-call | tf_op jit(solution)/shard_map/paste/pallas_call | solution.py:514

commit v4 on v3

--- a/solution.py
+++ b/solution.py
@@ -15,15 +15,16 @@
 TILES = 32
 CAP = 2
 FRAME = BANDS * STRIDE
-SENT = 56
+RIMMED = SPAN + 2
+SENT = 104
 MESH = pl.DeviceIdType.MESH
 BF = jnp.bfloat16
 F32 = jnp.float32
 CHUNK = 4
-U_DEC = 3
+U_DEC = 2
 U_CONV1 = 2
-U_CONV2 = 2
-U_PATCH = 8
+U_CONV2 = 4
+U_PATCH = 16
 VMEM_LIMIT = 60 * 1024 * 1024
 
 OFFSETS = sorted(
@@ -84,20 +85,25 @@
 def main_kernel(
     boxes,
     slots,
-    feat,
-    w0,
+    feat_in,
+    w0_in,
     b0,
-    w1,
+    w1_in,
     b1,
-    w2,
+    w2_in,
     b2,
     dec_out,
     rest_out,
     back,
+    feat,
+    w0,
+    w1,
+    w2,
     w0_pair,
     w1_pair,
     w2_pair,
     fpad,
+    stage,
     payload,
     got,
     reg,
@@ -113,6 +119,11 @@
     hpad,
     dwide,
     dec,
+    crop_tap,
+    crop_frac,
+    back_tap,
+    back_one,
+    back_two,
     fwd_send,
     fwd_recv,
     ret_send,
@@ -120,7 +131,13 @@
     halo_send,
     halo_recv,
     local_sem,
+    load_sem,
 ):
+    fetches = [
+        pltpu.make_async_copy(feat_in.at[b], feat.at[b], load_sem.at[3 + b]) for b in range(BANDS)
+    ]
+    for fetch in fetches:
+        fetch.start()
     me = lax.axis_index("tile")
     y, x, core = me // 8, (me // 2) % 4, me % 2
     targets = [
@@ -170,54 +187,94 @@
             remote(feat.at[:, 0], halo.at[1], halo_send.at[1], halo_recv.at[1], ahead),
         ]
 
+    loads = [
+        pltpu.make_async_copy(src, dst, load_sem.at[k])
+        for k, (src, dst) in enumerate(((w0_in, w0), (w1_in, w1), (w2_in, w2)))
+    ]
+    for load in loads:
+        load.start()
     fpad[:, 0:8, :] = jnp.zeros((2 * BANDS, 8, C), F32)
     fpad[:, COLS + 8 : COLS + 16, :] = jnp.zeros((2 * BANDS, 8, C), F32)
     for b in range(BANDS):
+        fetches[b].wait()
         for o in range(2):
             fpad[2 * b + o, 8 : COLS + 8, :] = feat[b, o].astype(F32)
 
-    def fill(s):
-        def body(w, _):
-            crop = jnp.maximum(slots[CAP * w + s], 0)
-            row0 = boxes[0, crop] - 1
-            col0 = boxes[1, crop]
-            parts = []
-            for i in range(2):
-                h = (2 * me + i - row0) & (STRIDE - 1)
-                band = jnp.clip((row0 + h) >> 6, 0, BANDS - 1)
-                parts.append(fpad[2 * band + i, pl.ds(col0 + 7, SENT), :])
-            payload[s, w] = jnp.concatenate(parts, axis=0).astype(BF)
-            return 0
-
-        lax.fori_loop(0, TILES, body, 0, unroll=2)
-
-    fill(0)
-    pl.semaphore_wait(barrier, PEERS)
-    for copy in forward(0):
+    def fill(s, w, spot):
+        crop = jnp.maximum(slots[CAP * w + s], 0)
+        row0 = boxes[0, crop] - 1
+        col0 = boxes[1, crop]
+        for i in range(2):
+            h = (2 * me + i - row0) & (STRIDE - 1)
+            band = jnp.clip((row0 + h) >> 6, 0, BANDS - 1)
+            stage[spot, pl.ds(i * RIMMED, 56), :] = fpad[2 * band + i, pl.ds(col0 + 7, 56), :]
+        payload[s, w] = stage[spot, 0:SENT].astype(BF)
+
+    ahead = forward(0)
+    step = 4
+    for k0 in range(0, PEERS + 1, step):
+        for k, w in enumerate((targets + [me])[k0 : k0 + step]):
+            fill(0, w, k)
+        if k0 == step:
+            pl.semaphore_wait(barrier, PEERS)
+        for copy in ahead[max(k0 - step, 0) : k0]:
+            copy.start()
+    for copy in ahead[PEERS + 1 - step :]:
         copy.start()
     own_forward(0).start()
-    fill(1)
-    for copy in forward(1):
-        copy.start()
-    own_forward(1).start()
-    for copy in rims():
-        copy.start()
-
+
+    def fill_next(j, _):
+        for k in range(4):
+            fill(1, 4 * j + k, k)
+        return 0
+
+    lax.fori_loop(0, TILES // 4, fill_next, 0)
+    for load in loads:
+        load.wait()
     pair_weight(w0, w0_pair)
     pair_weight(w1, w1_pair)
     pair_weight(w2, w2_pair)
     for ref in (wide, wide2):
         ref[0, 0] = jnp.zeros((S, 3 * C), BF)
         ref[S // 2, 1] = jnp.zeros((S, 3 * C), BF)
-    reg[STRIDE] = jnp.zeros((SENT, C), F32)
+    reg[TILES] = jnp.zeros((SENT, C), F32)
+    def taps(k, _):
+        crop = jnp.maximum(slots[CAP * me + k // S], 0)
+        side = UNIT * (boxes[2, crop] + 2)
+        t = k % S
+        num = jnp.clip((2 * t + 1) * side - S, 0, (side - 1) * 128)
+        crop_tap[k] = num >> 7
+        crop_frac[k] = (num & 127).astype(F32) * (1.0 / 128.0)
+        h = (t - boxes[0, crop]) & (STRIDE - 1)
+        magic = jnp.where(side == 24, 10923, jnp.where(side == 36, 7282, 5462))
+        inverse = jnp.where(side == 24, 1.0 / 24, jnp.where(side == 36, 1.0 / 36, 1.0 / 48))
+        num = jnp.clip((2 * h + 1) * (S // 2) - (side >> 1), 0, (S - 1) * side)
+        one = (num * magic) >> 18
+        frac = (num - one * side).astype(F32) * inverse
+        live = (h < side).astype(F32)
+        back_tap[k] = one
+        back_one[k] = live - live * frac
+        back_two[k] = live * frac
+        return 0
+
+    lax.fori_loop(0, CAP * S, taps, 0, unroll=4)
     hpad[:, 0:8, :] = jnp.zeros((2, 8, C), F32)
     hpad[:, COLS + 8 : COLS + 16, :] = jnp.zeros((2, 8, C), F32)
     bias0, bias1, bias2 = twice(b0), twice(b1), twice(b2)
 
-    def restore(s, _):
+    def arrived(s):
         own_forward(s).wait()
         for copy in forward(s):
             copy.wait_recv()
+
+    arrived(0)
+    for copy in forward(1):
+        copy.start()
+    own_forward(1).start()
+    for copy in rims():
+        copy.start()
+
+    def restore(s, _):
         slot = slots[CAP * me + s]
         crop = jnp.maximum(slot, 0)
         row0 = boxes[0, crop]
@@ -225,9 +282,7 @@
         sidef = side.astype(F32)
 
         def unpack(p, _):
-            block = got[s, p].astype(F32)
-            reg[2 * p] = block[0:SENT]
-            reg[2 * p + 1] = block[SENT : 2 * SENT]
+            reg[p] = got[s, p].astype(F32)
             return 0
 
         lax.fori_loop(0, TILES, unpack, 0, unroll=8)
@@ -236,8 +291,8 @@
             for o in range(2):
                 row = row0 - 1 + 2 * h + o
                 live = (row >= 0) & (row < FRAME)
-                index = jnp.where(live, row & (STRIDE - 1), STRIDE)
-                wide0[h, o] = widen(reg, index, 0, SPAN)
+                index = jnp.where(live, (row & (STRIDE - 1)) >> 1, TILES)
+                wide0[h, o] = widen(reg, index, (row & 1) * RIMMED, SPAN)
             return 0
 
         lax.fori_loop(0, SPAN // 2 + 1, region, 0, unroll=5)
@@ -269,10 +324,9 @@
         lax.fori_loop(0, SPAN // 2, colcut, 0, unroll=12)
 
         def crop_row(t, _):
-            num = jnp.clip((2 * t + 1) * side - S, 0, (side - 1) * 128)
-            first = num >> 7
+            first = crop_tap[s * S + t]
             second = jnp.minimum(first + 1, SPAN - 1)
-            frac = (num & 127).astype(F32) * (1.0 / 128.0)
+            frac = crop_frac[s * S + t]
             v = (1.0 - frac) * cut[first] + frac * cut[second]
             wide[(t + 1) >> 1, (t + 1) & 1] = spread_row(v)
             return 0
@@ -313,21 +367,13 @@
         lift_high = lift.astype(BF)
         lift_low = (lift - lift_high.astype(F32)).astype(BF)
         lifts = jnp.concatenate([lift_high, lift_low], axis=0)
-        magic = jnp.where(side == 24, 10923, jnp.where(side == 36, 7282, 5462))
-        inverse = jnp.where(side == 24, 1.0 / 24, jnp.where(side == 36, 1.0 / 36, 1.0 / 48))
-
         def patch(p):
             halves = []
             for i in range(2):
-                h = (2 * p + i - row0) & (STRIDE - 1)
-                num = jnp.clip((2 * h + 1) * (S // 2) - (side >> 1), 0, (S - 1) * side)
-                one = (num * magic) >> 18
-                frac = (num - one * side).astype(F32) * inverse
-                live = (h < side).astype(F32)
+                k = s * S + 2 * p + i
+                one = back_tap[k]
                 two = jnp.minimum(one + 1, S - 1)
-                halves.append(
-                    ((live - live * frac) * delta[one] + (live * frac) * delta[two]).astype(BF)
-                )
+                halves.append((back_one[k] * delta[one] + back_two[k] * delta[two]).astype(BF))
             rhs = jnp.concatenate(halves, axis=-1)
             z = jnp.dot(lifts, rhs, preferred_element_type=F32)
             z = (z[0:SPAN] + z[SPAN : 2 * SPAN]).astype(BF)
@@ -343,6 +389,11 @@
         for copy in copies[PEERS + 1 - U_PATCH :]:
             copy.start()
         own_backward(s).start()
+
+        @pl.when(s == 0)
+        def _():
+            arrived(1)
+
         return 0
 
     lax.fori_loop(0, CAP, restore, 0)
@@ -456,7 +507,9 @@
     dma = pltpu.SemaphoreType.DMA
     pair = pltpu.VMEM((12 * C, 2 * C), BF)
     spread = pltpu.VMEM((S // 2 + 1, 2, S, 3 * C), BF)
-    sent = pltpu.VMEM((CAP, TILES, 2 * SENT, C), BF)
+    table = (CAP * S,)
+    sent = pltpu.VMEM((CAP, TILES, SENT, C), BF)
+    weight = pltpu.VMEM((9, C, C), BF)
 
     decoded, rest, back = pl.pallas_call(
         main_kernel,
@@ -465,16 +518,21 @@
             rest_type,
             jax.ShapeDtypeStruct((CAP, TILES, 2, SPAN, C), BF),
         ),
-        in_specs=[smem, smem] + [vmem] * 7,
+        in_specs=[smem, smem, any_] + [any_, vmem] * 3,
         out_specs=(any_, any_, any_),
         scratch_shapes=[
+            pltpu.VMEM((BANDS, 2, COLS, C), BF),
+            weight,
+            weight,
+            weight,
             pair,
             pair,
             pair,
             pltpu.VMEM((2 * BANDS, COLS + 16, C), F32),
+            pltpu.VMEM((4, SENT + 8, C), F32),
             sent,
             sent,
-            pltpu.VMEM((STRIDE + 1, SENT, C), F32),
+            pltpu.VMEM((TILES + 1, SENT, C), F32),
             pltpu.VMEM((SPAN // 2 + 1, 2, SPAN, 3 * C), BF),
             pltpu.VMEM((SPAN // 2, SPAN, 2 * C), BF),
             pltpu.VMEM((SPAN, S, C), F32),
@@ -487,6 +545,11 @@
             pltpu.VMEM((2, COLS + 16, C), F32),
             pltpu.VMEM((4, COLS, 3 * C), BF),
             pltpu.VMEM((BANDS, 2, COLS, C), BF),
+            pltpu.SMEM(table, jnp.int32),
+            pltpu.SMEM(table, F32),
+            pltpu.SMEM(table, jnp.int32),
+            pltpu.SMEM(table, F32),
+            pltpu.SMEM(table, F32),
             dma((CAP, PEERS)),
             dma((CAP, PEERS)),
             dma((CAP, PEERS)),
@@ -494,6 +557,7 @@
             dma((2,)),
             dma((2,)),
             dma((7,)),
+            dma((3 + BANDS,)),
         ],
         compiler_params=pltpu.CompilerParams(
             collective_id=0, has_side_effects=True, vmem_limit_bytes=VMEM_LIMIT

time: 65.1 us -> 64.8 us (level)
  no operation moved by 1% of the time
where the time goes in v4:
time: 64.8 us; the launch traced here: 64.6 us
  Pallas kernels  64 us (99%)
    pallas_call x1, Pallas kernels, shards(): pl.pallas_call(main_kernel, out_shape=(frame_type, rest_type, jax.ShapeDt...  59.2 us
    pallas_call x1, Pallas kernels, shards(): pl.pallas_call(paste_kernel, out_shape=(frame_type, rest_type), in_specs=...  4.8 us

profile of v4, /device:TPU:1, one launch (start us, length us, event | category | flops | bytes accessed | tf_op | source)
XLA Modules:
  0.0 64.6 jit_solution(9613933408077229706)
XLA Ops:
  0.6 59.2 %main.1 = (bf16[6,2,320,128]{3,2,1,0:T(8,128)(2,1)}, bf16[2,64,64,128]{3,2,1,0:T(8,128)(2,1)}, bf16[2,32,2,48,128]{4,3,2,1,0:T(8,128)(2,1)}) custom-call(s32[3,32]{1,0:T(4,128)} %boxes.3, s32[64]{0:T(128)} %slots.3, bf16[6,2,320,128]{3,2,1,0:T(8,128)(2,1)} %feat_in.1, bf16[9,128,128]{2,1,0:T(8,128)(2,1)} %w0_in.1, f32[1,128]{1,0:T(1,128)} %bitcast.3, ...), custom_call_target="tpu_custom_call" | custom-call | tf_op jit(solution)/shard_map/main/pallas_call | solution.py:514
  59.8 4.8 %paste.1 = (bf16[6,2,320,128]{3,2,1,0:T(8,128)(2,1)}, bf16[2,64,64,128]{3,2,1,0:T(8,128)(2,1)}) custom-call(s32[3,32]{1,0:T(4,128)} %boxes.3, s32[64]{0:T(128)} %slots.3, bf16[6,2,320,128]{3,2,1,0:T(8,128)(2,1)} %get-tuple-element.5.dec_in, bf16[2,32,2,48,128]{4,3,2,1,0:T(8,128)(2,1)} %get-tuple-element.6.back_in, ...), custom_call_target="tpu_custom_call" | custom-call | tf_op jit(solution)/shard_map/paste/pallas_call | solution.py:578

commit v5 on v4

--- a/solution.py
+++ b/solution.py
@@ -24,7 +24,8 @@
 U_DEC = 2
 U_CONV1 = 2
 U_CONV2 = 4
-U_PATCH = 16
+U_PATCH = 8
+EARLY = 2
 VMEM_LIMIT = 60 * 1024 * 1024
 
 OFFSETS = sorted(
@@ -180,11 +181,18 @@
     def keep_rest(s):
         return pltpu.make_async_copy(rest.at[s], rest_out.at[s], local_sem.at[4 + s])
 
-    def rims():
+    def rims(part):
         after, ahead = (me + 1) % TILES, (me + TILES - 1) % TILES
+        bands = pl.ds(0, EARLY) if part == 0 else pl.ds(EARLY, BANDS - EARLY)
         return [
-            remote(feat.at[:, 1], halo.at[0], halo_send.at[0], halo_recv.at[0], after),
-            remote(feat.at[:, 0], halo.at[1], halo_send.at[1], halo_recv.at[1], ahead),
+            remote(
+                feat.at[bands, 1 - side],
+                halo.at[side, bands],
+                halo_send.at[part, side],
+                halo_recv.at[part, side],
+                t,
+            )
+            for side, t in enumerate((after, ahead))
         ]
 
     loads = [
@@ -217,6 +225,8 @@
             fill(0, w, k)
         if k0 == step:
             pl.semaphore_wait(barrier, PEERS)
+            for copy in rims(0):
+                copy.start()
         for copy in ahead[max(k0 - step, 0) : k0]:
             copy.start()
     for copy in ahead[PEERS + 1 - step :]:
@@ -267,12 +277,14 @@
         for copy in forward(s):
             copy.wait_recv()
 
-    arrived(0)
+    for copy in forward(0):
+        copy.wait_send()
     for copy in forward(1):
         copy.start()
     own_forward(1).start()
-    for copy in rims():
+    for copy in rims(1):
         copy.start()
+    arrived(0)
 
     def restore(s, _):
         slot = slots[CAP * me + s]
@@ -398,8 +410,9 @@
 
     lax.fori_loop(0, CAP, restore, 0)
 
-    for copy in rims():
-        copy.wait_recv()
+    for part in range(2):
+        for copy in rims(part):
+            copy.wait_recv()
 
     def band(b, _):
         up = jnp.where(me == 0, b - 1, b)
@@ -424,11 +437,12 @@
     lax.fori_loop(0, BANDS, band, 0)
     out = pltpu.make_async_copy(dec, dec_out, local_sem.at[6])
     out.start()
-    for copy in rims():
+    for part in range(2):
+        for copy in rims(part):
+            copy.wait_send()
+    for copy in forward(1):
         copy.wait_send()
     for s in range(CAP):
-        for copy in forward(s):
-            copy.wait_send()
         keep_rest(s).wait()
         own_backward(s).wait()
     for s in range(CAP):
@@ -441,18 +455,19 @@
     boxes, slots, dec_in, back_in, rest_in, out, rest_out, dec, back, rest, acc, done, sem
 ):
     position = lax.axis_index("tile")
-    fetch_dec = pltpu.make_async_copy(dec_in, dec, sem.at[0])
+    fetch_dec = [
+        pltpu.make_async_copy(dec_in.at[b], dec.at[b], sem.at[5 + BANDS + b]) for b in range(BANDS)
+    ]
     fetch_back = [
         pltpu.make_async_copy(back_in.at[s], back.at[s], sem.at[1 + s]) for s in range(CAP)
     ]
     fetch_rest = pltpu.make_async_copy(rest_in, rest, sem.at[3])
     store_rest = pltpu.make_async_copy(rest, rest_out, sem.at[4])
-    fetch_dec.start()
-    for copy in fetch_back:
+    for copy in fetch_dec + fetch_back:
         copy.start()
     fetch_rest.start()
-    fetch_dec.wait()
     for b in range(BANDS):
+        fetch_dec[b].wait()
         for o in range(2):
             acc[2 * b + o] = dec[b, o].astype(F32)
 
@@ -466,10 +481,13 @@
             def _():
                 row0 = boxes[0, slot]
                 cols = pl.ds(boxes[1, slot], SPAN)
+                rows, sums = [], []
                 for i in range(2):
                     h = (2 * position + i - row0) & (STRIDE - 1)
-                    row = jnp.where(h < SPAN, 2 * ((row0 + h) >> 6) + i, 2 * BANDS + i)
-                    acc[row, cols, :] = acc[row, cols, :] + back[s, w, i].astype(F32)
+                    rows.append(jnp.where(h < SPAN, 2 * ((row0 + h) >> 6) + i, 2 * BANDS + i))
+                    sums.append(acc[rows[i], cols, :] + back[s, w, i].astype(F32))
+                for i in range(2):
+                    acc[rows[i], cols, :] = sums[i]
 
             return 0
 
@@ -554,8 +572,8 @@
             dma((CAP, PEERS)),
             dma((CAP, PEERS)),
             dma((CAP, PEERS)),
-            dma((2,)),
-            dma((2,)),
+            dma((2, 2)),
+            dma((2, 2)),
             dma((7,)),
             dma((3 + BANDS,)),
         ],
@@ -586,7 +604,7 @@
             pltpu.VMEM((CAP, S, S, C), BF),
             pltpu.VMEM((2 * BANDS + 2, COLS, C), F32),
             pltpu.VMEM((BANDS, 2, COLS, C), BF),
-            dma((5 + BANDS,)),
+            dma((5 + 2 * BANDS,)),
         ],
         compiler_params=pltpu.CompilerParams(vmem_limit_bytes=VMEM_LIMIT),
         name="paste",

time: 64.8 us -> 63.5 us (0.980)
  Pallas kernels: 64 us -> 62.7 us
    pallas_call x1, Pallas kernels: 59.2 us -> 57.7 us  [shards(): pl.pallas_call(main_kernel, out_shape=(frame_type, rest_type, jax.ShapeDt...]
where the time goes in v5:
time: 63.5 us; the launch traced here: 63.3 us
  Pallas kernels  62.7 us (99%)
  between operations  0.64 us (1%)
    pallas_call x1, Pallas kernels, shards(): pl.pallas_call(main_kernel, out_shape=(frame_type, rest_type, jax.ShapeDt...  57.7 us
    pallas_call x1, Pallas kernels, shards(): pl.pallas_call(paste_kernel, out_shape=(frame_type, rest_type), in_specs=...  4.98 us

profile of v5, /device:TPU:1, one launch (start us, length us, event | category | flops | bytes accessed | tf_op | source)
XLA Modules:
  0.0 63.3 jit_solution(10173622500086839571)
XLA Ops:
  0.6 57.7 %main.1 = (bf16[6,2,320,128]{3,2,1,0:T(8,128)(2,1)}, bf16[2,64,64,128]{3,2,1,0:T(8,128)(2,1)}, bf16[2,32,2,48,128]{4,3,2,1,0:T(8,128)(2,1)}) custom-call(s32[3,32]{1,0:T(4,128)} %boxes.3, s32[64]{0:T(128)} %slots.3, bf16[6,2,320,128]{3,2,1,0:T(8,128)(2,1)} %feat_in.1, bf16[9,128,128]{2,1,0:T(8,128)(2,1)} %w0_in.1, f32[1,128]{1,0:T(1,128)} %bitcast.3, ...), custom_call_target="tpu_custom_call" | custom-call | tf_op jit(solution)/shard_map/main/pallas_call | solution.py:532
  58.3 5.0 %paste.1 = (bf16[6,2,320,128]{3,2,1,0:T(8,128)(2,1)}, bf16[2,64,64,128]{3,2,1,0:T(8,128)(2,1)}) custom-call(s32[3,32]{1,0:T(4,128)} %boxes.3, s32[64]{0:T(128)} %slots.3, bf16[6,2,320,128]{3,2,1,0:T(8,128)(2,1)} %get-tuple-element.5.dec_in, bf16[2,32,2,48,128]{4,3,2,1,0:T(8,128)(2,1)} %get-tuple-element.6.back_in, ...), custom_call_target="tpu_custom_call" | custom-call | tf_op jit(solution)/shard_map/paste/pallas_call | solution.py:596

commit v6 on v5

--- a/solution.py
+++ b/solution.py
@@ -25,7 +25,7 @@
 U_CONV1 = 2
 U_CONV2 = 4
 U_PATCH = 8
-EARLY = 2
+EARLY = 1
 VMEM_LIMIT = 60 * 1024 * 1024
 
 OFFSETS = sorted(
@@ -455,19 +455,18 @@
     boxes, slots, dec_in, back_in, rest_in, out, rest_out, dec, back, rest, acc, done, sem
 ):
     position = lax.axis_index("tile")
-    fetch_dec = [
-        pltpu.make_async_copy(dec_in.at[b], dec.at[b], sem.at[5 + BANDS + b]) for b in range(BANDS)
-    ]
+    fetch_dec = pltpu.make_async_copy(dec_in, dec, sem.at[0])
     fetch_back = [
         pltpu.make_async_copy(back_in.at[s], back.at[s], sem.at[1 + s]) for s in range(CAP)
     ]
     fetch_rest = pltpu.make_async_copy(rest_in, rest, sem.at[3])
     store_rest = pltpu.make_async_copy(rest, rest_out, sem.at[4])
-    for copy in fetch_dec + fetch_back:
+    fetch_dec.start()
+    for copy in fetch_back:
         copy.start()
     fetch_rest.start()
+    fetch_dec.wait()
     for b in range(BANDS):
-        fetch_dec[b].wait()
         for o in range(2):
             acc[2 * b + o] = dec[b, o].astype(F32)
 
@@ -481,13 +480,10 @@
             def _():
                 row0 = boxes[0, slot]
                 cols = pl.ds(boxes[1, slot], SPAN)
-                rows, sums = [], []
                 for i in range(2):
                     h = (2 * position + i - row0) & (STRIDE - 1)
-                    rows.append(jnp.where(h < SPAN, 2 * ((row0 + h) >> 6) + i, 2 * BANDS + i))
-                    sums.append(acc[rows[i], cols, :] + back[s, w, i].astype(F32))
-                for i in range(2):
-                    acc[rows[i], cols, :] = sums[i]
+                    row = jnp.where(h < SPAN, 2 * ((row0 + h) >> 6) + i, 2 * BANDS + i)
+                    acc[row, cols, :] = acc[row, cols, :] + back[s, w, i].astype(F32)
 
             return 0
 
@@ -604,7 +600,7 @@
             pltpu.VMEM((CAP, S, S, C), BF),
             pltpu.VMEM((2 * BANDS + 2, COLS, C), F32),
             pltpu.VMEM((BANDS, 2, COLS, C), BF),
-            dma((5 + 2 * BANDS,)),
+            dma((5 + BANDS,)),
         ],
         compiler_params=pltpu.CompilerParams(vmem_limit_bytes=VMEM_LIMIT),
         name="paste",

time: 63.5 us -> 65.1 us (1.025)
  the two profiles are of different devices: /device:TPU:1 before, /device:TPU:4 now
where the time goes in v6:
time: 65.1 us; the launch traced here: 64.9 us
  Pallas kernels  64.2 us (99%)
    pallas_call x1, Pallas kernels, shards(): pl.pallas_call(main_kernel, out_shape=(frame_type, rest_type, jax.ShapeDt...  59.4 us
    pallas_call x1, Pallas kernels, shards(): pl.pallas_call(paste_kernel, out_shape=(frame_type, rest_type), in_specs=...  4.8 us

profile of v6, /device:TPU:4, one launch (start us, length us, event | category | flops | bytes accessed | tf_op | source)
XLA Modules:
  0.0 64.9 jit_solution(1406775158580633139)
XLA Ops:
  0.6 59.4 %main.1 = (bf16[6,2,320,128]{3,2,1,0:T(8,128)(2,1)}, bf16[2,64,64,128]{3,2,1,0:T(8,128)(2,1)}, bf16[2,32,2,48,128]{4,3,2,1,0:T(8,128)(2,1)}) custom-call(s32[3,32]{1,0:T(4,128)} %boxes.3, s32[64]{0:T(128)} %slots.3, bf16[6,2,320,128]{3,2,1,0:T(8,128)(2,1)} %feat_in.1, bf16[9,128,128]{2,1,0:T(8,128)(2,1)} %w0_in.1, f32[1,128]{1,0:T(1,128)} %bitcast.3, ...), custom_call_target="tpu_custom_call" | custom-call | tf_op jit(solution)/shard_map/main/pallas_call | solution.py:528
  60.1 4.8 %paste.1 = (bf16[6,2,320,128]{3,2,1,0:T(8,128)(2,1)}, bf16[2,64,64,128]{3,2,1,0:T(8,128)(2,1)}) custom-call(s32[3,32]{1,0:T(4,128)} %boxes.3, s32[64]{0:T(128)} %slots.3, bf16[6,2,320,128]{3,2,1,0:T(8,128)(2,1)} %get-tuple-element.5.dec_in, bf16[2,32,2,48,128]{4,3,2,1,0:T(8,128)(2,1)} %get-tuple-element.6.back_in, ...), custom_call_target="tpu_custom_call" | custom-call | tf_op jit(solution)/shard_map/paste/pallas_call | solution.py:592

commit v7 on v6

--- a/solution.py
+++ b/solution.py
@@ -25,7 +25,7 @@
 U_CONV1 = 2
 U_CONV2 = 4
 U_PATCH = 8
-EARLY = 1
+EARLY = 3
 VMEM_LIMIT = 60 * 1024 * 1024
 
 OFFSETS = sorted(

time: 65.1 us -> 65 us (level)
  the two profiles are of different devices: /device:TPU:4 before, /device:TPU:1 now
where the time goes in v7:
time: 65 us; the launch traced here: 64.8 us
  Pallas kernels  64.1 us (99%)
    pallas_call x1, Pallas kernels, shards(): pl.pallas_call(main_kernel, out_shape=(frame_type, rest_type, jax.ShapeDt...  59.3 us
    pallas_call x1, Pallas kernels, shards(): pl.pallas_call(paste_kernel, out_shape=(frame_type, rest_type), in_specs=...  4.8 us

profile of v7, /device:TPU:1, one launch (start us, length us, event | category | flops | bytes accessed | tf_op | source)
XLA Modules:
  0.0 64.8 jit_solution(933571065821897897)
XLA Ops:
  0.6 59.3 %main.1 = (bf16[6,2,320,128]{3,2,1,0:T(8,128)(2,1)}, bf16[2,64,64,128]{3,2,1,0:T(8,128)(2,1)}, bf16[2,32,2,48,128]{4,3,2,1,0:T(8,128)(2,1)}) custom-call(s32[3,32]{1,0:T(4,128)} %boxes.3, s32[64]{0:T(128)} %slots.3, bf16[6,2,320,128]{3,2,1,0:T(8,128)(2,1)} %feat_in.1, bf16[9,128,128]{2,1,0:T(8,128)(2,1)} %w0_in.1, f32[1,128]{1,0:T(1,128)} %bitcast.3, ...), custom_call_target="tpu_custom_call" | custom-call | tf_op jit(solution)/shard_map/main/pallas_call | solution.py:528
  60.0 4.8 %paste.1 = (bf16[6,2,320,128]{3,2,1,0:T(8,128)(2,1)}, bf16[2,64,64,128]{3,2,1,0:T(8,128)(2,1)}) custom-call(s32[3,32]{1,0:T(4,128)} %boxes.3, s32[64]{0:T(128)} %slots.3, bf16[6,2,320,128]{3,2,1,0:T(8,128)(2,1)} %get-tuple-element.5.dec_in, bf16[2,32,2,48,128]{4,3,2,1,0:T(8,128)(2,1)} %get-tuple-element.6.back_in, ...), custom_call_target="tpu_custom_call" | custom-call | tf_op jit(solution)/shard_map/paste/pallas_call | solution.py:592
